TPU v7x, 32 devices: a whole 2x2x4 slice. The times are simulated.
32 devices in a mesh: tgt: 4 (over y, core), blk: 8 (over z, x).
Axes of the slice: x: 2, y: 2, z: 4, core: 2. Of those that a mesh axis runs over, the one named last changes fastest.
Arguments:
- integrals: bfloat16 [8192, 128, 128], P(('tgt', 'blk')), may hold values from -0.5 to 0.5
- densities: bfloat16 [60, 128, 128], P('tgt'), may hold values from -1.5 to 1.5
- entry_block: int32 [65536], P(('tgt', 'blk')), may hold values from 0 to 255
- entry_state: int32 [65536], P(('tgt', 'blk')), may hold values from 0 to 59, as said below
- entry_slot: int32 [65536], P(('tgt', 'blk')), may hold values from 0 to 127
- counts: int32 [32, 4], P(('tgt', 'blk')), may hold values from 0 to 2048, as said below
- owner: int32 [1024], P('blk'), may hold values from 0 to 1023, as said below
Outputs:
- hamiltonian: float32 [1024, 128, 128], P(('tgt', 'blk'))
Inputs may be any that keep to these rules, and one draw needn't show every extreme that they name: `counts`: each row sums to at most 2048; on some device all 2048 slots are live and belong to a single group of target states. `entry_state`: within each device's slots, the first counts[d, 0] name states of group 0 (states 0 to 14), the next counts[d, 1] states of group 1, and so on; the slots after the live ones are unused. `owner`: A permutation of 0 to 1023; output positions d * 32 to (d + 1) * 32 - 1 belong to device d, and of the 128 blocks of one block-row group exactly 4 go to each device.
All inputs are finite; a program needn't handle non-finite values.
Results may differ from a plain program's by a relative error of at most 0.0003.
Values may be sent and summed in bfloat16 or wider, within the bound.
A program may use at most 128 MiB of HBM per device.

v0:
```python
import jax
import jax.numpy as jnp
from jax import lax
from jax.experimental import pallas as pl
from jax.experimental.pallas import tpu as pltpu
from jax.sharding import PartitionSpec as P

CHUNK = 4
UNROLL = 2


def bits_for(n):
    return max(1, (n - 1).bit_length())


def accumulate(n_steps, keys, place, integrals, densities, st_bits, blk_bits, hb_rows):
    states, size, _ = densities.shape
    held = integrals.shape[0]
    st_mask = (1 << st_bits) - 1
    blk_mask = (1 << blk_bits) - 1

    def kernel(n_ref, keys_ref, place_ref, int_hbm, den_hbm, out_hbm, ints, dens, acc, sems):
        load_ints = pltpu.make_async_copy(int_hbm, ints, sems.at[0])
        load_dens = pltpu.make_async_copy(den_hbm, dens.at[pl.ds(0, states)], sems.at[1])
        load_ints.start()
        load_dens.start()
        dens[states] = jnp.zeros((size, size), dens.dtype)

        @pl.loop(0, hb_rows)
        def _(j):
            acc[j] = jnp.zeros((size, size), jnp.float32)

        load_ints.wait()
        load_dens.wait()

        @pl.loop(0, n_ref[0])
        def _(step):
            prods = []
            for u in range(UNROLL):
                base = (step * UNROLL + u) * CHUNK
                ks = [keys_ref[base + i] for i in range(CHUNK)]
                lhs = jnp.concatenate([ints[(k >> st_bits) & blk_mask] for k in ks], axis=1)
                rhs = jnp.concatenate([dens[k & st_mask] for k in ks], axis=0)
                row = place_ref[ks[0] >> (st_bits + blk_bits)]
                prods.append((row, jnp.dot(lhs, rhs, preferred_element_type=jnp.float32)))
            for row, prod in prods:
                acc[row] += prod

        store = pltpu.make_async_copy(acc, out_hbm, sems.at[2])
        store.start()
        store.wait()

    smem = pl.BlockSpec(memory_space=pltpu.SMEM)
    hbm = pl.BlockSpec(memory_space=pl.ANY)
    return pl.pallas_call(
        kernel,
        out_shape=jax.ShapeDtypeStruct((hb_rows, size, size), jnp.float32),
        in_specs=[smem, smem, smem, hbm, hbm],
        out_specs=hbm,
        scratch_shapes=[
            pltpu.VMEM((held, size, size), integrals.dtype),
            pltpu.VMEM((states + 1, size, size), densities.dtype),
            pltpu.VMEM((hb_rows, size, size), jnp.float32),
            pltpu.SemaphoreType.DMA((3,)),
        ],
        compiler_params=pltpu.CompilerParams(vmem_limit_bytes=40 << 20),
    )(n_steps, keys, place, integrals, densities)


def make_keys(entry_block, entry_state, entry_slot, live, hb_rows, held, states):
    st_bits = bits_for(states + 1)
    blk_bits = bits_for(held)
    e_cap = entry_block.shape[0]
    valid = jnp.arange(e_cap, dtype=jnp.int32) < live
    slots = jnp.arange(hb_rows, dtype=jnp.int32)
    per_slot = jnp.sum(
        ((entry_slot[:, None] == slots[None, :]) & valid[:, None]).astype(jnp.int32), axis=0
    )
    spare = (-per_slot) % CHUNK
    filler = (slots << (st_bits + blk_bits)) + ((held - 1) << st_bits) + states
    last = filler[hb_rows - 1]
    key = (((entry_slot << blk_bits) + entry_block) << st_bits) + entry_state
    key = jnp.where(valid, key, last)
    order = jnp.arange(CHUNK - 1, dtype=jnp.int32)
    fill = jnp.where(order[:, None] < spare[None, :], filler[None, :], last).reshape(-1)
    total = e_cap + fill.shape[0]
    group = CHUNK * UNROLL
    tail = jnp.full(((-total) % group,), last, jnp.int32)
    keys = lax.sort(jnp.concatenate([key, fill, tail]))
    n_steps = (jnp.sum(per_slot + spare) + group - 1) // group
    return keys, n_steps.reshape(1), st_bits, blk_bits


def on_device(integrals, densities, entry_block, entry_state, entry_slot, counts, owner):
    size = integrals.shape[1]
    hb_rows = owner.shape[0]
    n_tgt = lax.axis_size("tgt")
    n_blk = lax.axis_size("blk")
    own_rows = hb_rows // n_tgt
    piece = lax.all_gather(densities, "tgt", axis=0, tiled=True)
    keys, n_steps, st_bits, blk_bits = make_keys(
        entry_block, entry_state, entry_slot, jnp.sum(counts[0]), hb_rows,
        integrals.shape[0], piece.shape[0],
    )
    place = jnp.sum((owner[None, :] < owner[:, None]).astype(jnp.int32), axis=1)
    partial = accumulate(n_steps, keys, place, integrals, piece, st_bits, blk_bits, hb_rows)
    mine = lax.psum_scatter(partial, "tgt", scatter_dimension=0, tiled=True)
    sorted_owner = lax.sort(owner)
    pos = lax.dynamic_slice_in_dim(sorted_owner, lax.axis_index("tgt") * own_rows, own_rows)
    got = lax.all_to_all(mine, "blk", split_axis=0, concat_axis=0, tiled=True)
    got_pos = lax.all_to_all(pos, "blk", split_axis=0, concat_axis=0, tiled=True)
    return got[jnp.argsort(got_pos)]


def solution(mesh):
    in_specs = (
        P(("tgt", "blk"), None, None),
        P("tgt", None, None),
        P(("tgt", "blk")),
        P(("tgt", "blk")),
        P(("tgt", "blk")),
        P(("tgt", "blk"), None),
        P("blk"),
    )
    out_specs = P(("tgt", "blk"), None, None)
    return jax.shard_map(
        on_device, mesh=mesh, in_specs=in_specs, out_specs=out_specs, check_vma=False
    )
```

profile of v0, /device:TPU:11, one launch (start us, length us, event | category | flops | bytes accessed | tf_op | source)
XLA Modules:
  0.0 235.5 jit_solution(6585862115297147852)
XLA Ops:
  6.5 0.7 all-gather.2.cloned.1.call-update
  7.3 1.3 reduce_sum.36
  8.6 0.7 iota_compare_fusion.1
  9.3 2.6 %convert_reduce_fusion = s32[128]{0:T(128)S(1)} fusion(s32[2048]{0:T(1024)} %param.11, pred[2048]{0:T(1024)(128)(4,1)S(1)} %iota_compare_fusion.1), kind=kLoop, calls=%fused_computation.1 | loop fusion | flops 1048448 | bytes 10752 | tf_op jit(solution)/shard_map/reduce_sum | solution.py:76
  11.9 0.7 add_reduce_fusion
  13.2 0.6 slice.3
  13.8 0.6 select_bitcast_fusion
  14.5 2.0 add_select_fusion
  16.5 5.8 %sort.44 = (s32[2432]{0:T(1024)S(1)}, s32[2432]{0:T(1024)}) sort(s32[2432]{0:T(1024)S(1)} %pad_add_fusion, s32[2432]{0:T(1024)S(1)} %iota.31), dimensions={0}, to_apply=%region_3.4 | sort | flops 29184 | bytes 38912 | tf_op jit(solution)/shard_map/sort | solution.py:89
  22.3 0.9 convert_reduce_fusion.1.place_ref
  23.2 9.3 %all-gather.2.cloned.1.call-done.den_hbm = bf16[60,128,128]{2,1,0:T(8,128)(2,1)} async-done(((bf16[15,128,128]{2,1,0:T(8,128)(2,1)}), bf16[60,128,128]{2,1,0:T(8,128)(2,1)}) %all-gather.2.cloned.1.call-update) | async-done | bytes 1966096 | tf_op jit(solution)/shard_map/all_gather | solution.py:100
  32.5 1.5 copy-done.1
  34.0 19.9 %shard_map.73 = f32[128,128,128]{2,1,0:T(8,128)S(1)} custom-call(s32[1]{0:T(128)} %bitcast.n_ref, s32[2432]{0:T(1024)S(1)} %get-tuple-element.10.keys_ref, s32[128]{0:T(128)S(1)} %convert_reduce_fusion.1.place_ref, bf16[256,128,128]{2,1,0:T(8,128)(2,1)} %int_hbm.1, bf16[60,128,128]{2,1,0:T(8,128)(2,1)S(1)} %copy-done.1), custom_call_target="tpu_custom_call" | custom-call | tf_op jit(solution)/shard_map/pallas_call | solution.py:55
  53.9 3.2 %copy-done = f32[128,128,128]{2,1,0:T(8,128)} copy-done((f32[128,128,128]{2,1,0:T(8,128)}, f32[128,128,128]{2,1,0:T(8,128)S(1)}, u32[]{:S(2)}) %copy-start) | copy-done | bytes 8388632
  57.2 0.6 copy-done.2
  57.8 2.5 %sort.45 = (s32[128]{0:T(128)S(1)}, s32[128]{0:T(128)}) sort(s32[128]{0:T(128)S(1)} %copy-done.2, s32[128]{0:T(128)S(1)} %iota.32), dimensions={0}, to_apply=%region_6.7 | sort | flops 896 | bytes 2048 | tf_op jit(solution)/shard_map/sort | solution.py:108
  60.5 55.5 %all_to_all.17 = s32[8,4,1]{1,2,0:T(1,128)S(1)} all-to-all(s32[8,4,1]{1,2,0:T(1,128)S(1)} %bitcast.6), channel_id=1, replica_groups=mesh['tgt'=4,'blk'=8] {'blk'}, dimensions={0} | all-to-all | bytes 256 | tf_op jit(solution)/shard_map/all_to_all | solution.py:111
  116.0 59.5 %reduce-scatter.2.cloned.1.call-done = f32[32,128,128]{2,1,0:T(8,128)} async-done(((f32[128,128,128]{2,1,0:T(8,128)}), f32[32,128,128]{2,1,0:T(8,128)}) %reduce-scatter.2.cloned.1.call-update) | async-done | bytes 2097168 | tf_op jit(solution)/shard_map/reduce_scatter | solution.py:107
  175.5 5.5 %all-to-all-start = ((f32[32,128,128]{2,1,0:T(8,128)}), f32[32,128,128]{2,1,0:T(8,128)S(1)}, u32[]{:S(2)}, u32[]{:S(2)}) async-start(f32[32,128,128]{2,1,0:T(8,128)} %reduce-scatter.2.cloned.1.call-done), calls=%async_computation.1 | async-start | bytes 4194304 | tf_op jit(solution)/shard_map/all_to_all | solution.py:110
  180.9 0.5 broadcast.59
  181.5 0.7 reduce.4
  182.2 1.6 sort.46
  183.8 42.8 %all-to-all-done = f32[32,128,128]{2,1,0:T(8,128)S(1)} async-done(((f32[32,128,128]{2,1,0:T(8,128)}), f32[32,128,128]{2,1,0:T(8,128)S(1)}, u32[]{:S(2)}, u32[]{:S(2)}) %all-to-all-start) | async-done | bytes 2097184 | tf_op jit(solution)/shard_map/all_to_all | solution.py:110
  226.7 2.0 gather_fusion
  (15 shorter events, 0.3 us)
Async XLA Ops:
  6.5 25.9 %all-gather.2.cloned.1.call-start = ((), (), s32[]{:S(2)}) async-start(), calls=%async_computation.3 | async-start | bytes 2457600 | tf_op jit(solution)/shard_map/all_gather | solution.py:100
  7.3 168.2 %reduce-scatter.2.cloned.1.call-start = ((), (), s32[]{:S(2)}) async-start(), calls=%async_computation.4 | async-start | bytes 10485760 | tf_op jit(solution)/shard_map/reduce_scatter | solution.py:107
  32.5 1.5 copy-start.1
  53.9 3.2 %copy-start = (f32[128,128,128]{2,1,0:T(8,128)}, f32[128,128,128]{2,1,0:T(8,128)S(1)}, u32[]{:S(2)}) copy-start(f32[128,128,128]{2,1,0:T(8,128)S(1)} %shard_map.73) | copy-start | bytes 25165828
  57.1 0.7 copy-start.2
  175.5 51.2 %all-to-all-start = ((f32[32,128,128]{2,1,0:T(8,128)}), f32[32,128,128]{2,1,0:T(8,128)S(1)}, u32[]{:S(2)}, u32[]{:S(2)}) async-start(f32[32,128,128]{2,1,0:T(8,128)} %reduce-scatter.2.cloned.1.call-done), calls=%async_computation.1 | async-start | bytes 4194304 | tf_op jit(solution)/shard_map/all_to_all | solution.py:110
Sparse Core Ops, SparseCore 0:
  8.9 23.4 all-gather.1
  57.3 118.1 reduce-scatter.1
where the time goes:
time: 239 us; the launch traced here: 235 us
  waiting for transfers between devices  112 us (47%)
  blocking collectives  55.5 us (23%)
  Pallas kernels  19.9 us (8%)
  other arithmetic  19.3 us (8%)
  between operations  14.1 us (6%)
  local copies, waits for them, and re-layouts  8.77 us (4%)
  starting transfers between devices  5.5 us (2%)
    reduce_scatter x1, waiting for transfers between devices, on_device(): mine = lax.psum_scatter(partial, 'tgt', scatter_dimension=0, tiled=True)  59.5 us
    all_to_all x1, blocking collectives, on_device(): lax.all_to_all(pos, 'blk', split_axis=0, concat_axis=0, tiled=True)  55.5 us
    all_to_all x1, waiting for transfers between devices, on_device(): got = lax.all_to_all(mine, 'blk', split_axis=0, concat_axis=0, tiled=True)  42.8 us
    pallas_call x1, Pallas kernels, accumulate(): pl.pallas_call(kernel, out_shape=jax.ShapeDtypeStruct((hb_rows, size, siz...  19.9 us
    all_gather x1, waiting for transfers between devices, on_device(): piece = lax.all_gather(densities, 'tgt', axis=0, tiled=True)  9.29 us
    sort x1, other arithmetic, make_keys(): keys = lax.sort(jnp.concatenate([key, fill, tail]))  5.76 us
    all_to_all x1, starting transfers between devices, on_device(): got = lax.all_to_all(mine, 'blk', split_axis=0, concat_axis=0, tiled=True)  5.46 us
    unnamed x6, local copies, waits for them, and re-layouts  5.37 us
  transfers between devices with their start and end apart: 3, of which 3 were waited for; matrix products, arithmetic and copies ran while one was open for 9% of the time, Pallas kernels for 0%

commit v1 on v0

--- a/solution.py
+++ b/solution.py
@@ -7,6 +7,9 @@
 
 CHUNK = 4
 UNROLL = 2
+STEPS = 8
+LAG = 1
+MESH = pl.DeviceIdType.MESH
 
 
 def bits_for(n):
@@ -19,7 +22,7 @@
     st_mask = (1 << st_bits) - 1
     blk_mask = (1 << blk_bits) - 1
 
-    def kernel(n_ref, keys_ref, place_ref, int_hbm, den_hbm, out_hbm, ints, dens, acc, sems):
+    def kernel(n_ref, keys_ref, place_ref, int_hbm, den_hbm, acc, ints, dens, sems):
         load_ints = pltpu.make_async_copy(int_hbm, ints, sems.at[0])
         load_dens = pltpu.make_async_copy(den_hbm, dens.at[pl.ds(0, states)], sems.at[1])
         load_ints.start()
@@ -46,22 +49,17 @@
             for row, prod in prods:
                 acc[row] += prod
 
-        store = pltpu.make_async_copy(acc, out_hbm, sems.at[2])
-        store.start()
-        store.wait()
-
     smem = pl.BlockSpec(memory_space=pltpu.SMEM)
     hbm = pl.BlockSpec(memory_space=pl.ANY)
     return pl.pallas_call(
         kernel,
         out_shape=jax.ShapeDtypeStruct((hb_rows, size, size), jnp.float32),
         in_specs=[smem, smem, smem, hbm, hbm],
-        out_specs=hbm,
+        out_specs=pl.BlockSpec(memory_space=pltpu.VMEM),
         scratch_shapes=[
             pltpu.VMEM((held, size, size), integrals.dtype),
             pltpu.VMEM((states + 1, size, size), densities.dtype),
-            pltpu.VMEM((hb_rows, size, size), jnp.float32),
-            pltpu.SemaphoreType.DMA((3,)),
+            pltpu.SemaphoreType.DMA((2,)),
         ],
         compiler_params=pltpu.CompilerParams(vmem_limit_bytes=40 << 20),
     )(n_steps, keys, place, integrals, densities)
@@ -91,12 +89,187 @@
     return keys, n_steps.reshape(1), st_bits, blk_bits
 
 
+def exchange(partial, pos, own_rows, n_blk):
+    size = partial.shape[-1]
+    steps = min(STEPS, n_blk)
+    rows = own_rows // steps
+    dests = n_blk // steps
+    per = own_rows // n_blk
+
+    def kernel(part, pos_ref, out, pos_out, r1, s2, r2, mine,
+               s1_send, s1_recv, s2_send, s2_recv, s3_send, s3_recv, p_send, p_recv, own_sem):
+        t = lax.axis_index("tgt")
+        b = lax.axis_index("blk")
+        y, c = t // 2, t % 2
+        sibling = y * 2 + (1 - c)
+        across = (1 - y) * 2 + c
+        barrier = pltpu.get_barrier_semaphore()
+        pl.semaphore_signal(barrier, inc=1, device_id={"tgt": sibling}, device_id_type=MESH)
+        pl.semaphore_signal(barrier, inc=1, device_id={"tgt": across}, device_id_type=MESH)
+        for i in range(1, n_blk):
+            pl.semaphore_signal(
+                barrier, inc=1, device_id={"blk": (b + i) % n_blk}, device_id_type=MESH
+            )
+        pl.semaphore_wait(barrier, n_blk + 1)
+
+        def span(i):
+            return ((b // dests + 1 + i) % steps) * rows
+
+        def first(i, far):
+            side = 1 - y if far else y
+            return pltpu.make_async_remote_copy(
+                src_ref=part.at[pl.ds((side * 2 + 1 - c) * own_rows + span(i), rows)],
+                dst_ref=r1.at[far, pl.ds(span(i), rows)],
+                send_sem=s1_send.at[far, i],
+                recv_sem=s1_recv.at[far, i],
+                device_id={"tgt": sibling},
+                device_id_type=MESH,
+            )
+
+        def second(i):
+            return pltpu.make_async_remote_copy(
+                src_ref=s2.at[pl.ds(span(i), rows)],
+                dst_ref=r2.at[pl.ds(span(i), rows)],
+                send_sem=s2_send.at[i],
+                recv_sem=s2_recv.at[i],
+                device_id={"tgt": across},
+                device_id_type=MESH,
+            )
+
+        def third(dest):
+            return pltpu.make_async_remote_copy(
+                src_ref=mine.at[pl.ds(dest * per, per)],
+                dst_ref=out.at[pl.ds(b * per, per)],
+                send_sem=s3_send.at[dest],
+                recv_sem=s3_recv.at[b],
+                device_id={"blk": dest},
+                device_id_type=MESH,
+            )
+
+        def third_in(src):
+            return pltpu.make_async_remote_copy(
+                src_ref=mine.at[pl.ds(src * per, per)],
+                dst_ref=out.at[pl.ds(src * per, per)],
+                send_sem=s3_send.at[src],
+                recv_sem=s3_recv.at[src],
+                device_id={"blk": src},
+                device_id_type=MESH,
+            )
+
+        def places(dest, slot):
+            return pltpu.make_async_remote_copy(
+                src_ref=pos_ref.at[dest],
+                dst_ref=pos_out.at[slot],
+                send_sem=p_send.at[dest],
+                recv_sem=p_recv.at[slot],
+                device_id={"blk": dest},
+                device_id_type=MESH,
+            )
+
+        own_out = pltpu.make_async_copy(
+            mine.at[pl.ds(b * per, per)], out.at[pl.ds(b * per, per)], own_sem.at[0]
+        )
+        own_pos = pltpu.make_async_copy(pos_ref.at[b], pos_out.at[b], own_sem.at[1])
+
+        for i in range(steps):
+            first(i, 1).start()
+            first(i, 0).start()
+        own_pos.start()
+        for i in range(1, n_blk):
+            places((b + i) % n_blk, b).start()
+
+        def dest_of(i, j):
+            return ((b // dests + 1 + i) % steps) * dests + (b % dests + j) % dests
+
+        def finish(i):
+            second(i).wait_recv()
+            at = pl.ds(span(i), rows)
+            mine[at] = mine[at] + r2[at]
+            for j in range(dests):
+                if i == steps - 1 and j == 0:
+                    own_out.start()
+                else:
+                    third(dest_of(i, j)).start()
+
+        for i in range(steps):
+            at = pl.ds(span(i), rows)
+            first(i, 1).wait_recv()
+            s2[at] = part[pl.ds(((1 - y) * 2 + c) * own_rows + span(i), rows)] + r1[1, at]
+            second(i).start()
+            first(i, 0).wait_recv()
+            mine[at] = part[pl.ds((y * 2 + c) * own_rows + span(i), rows)] + r1[0, at]
+            if i >= LAG:
+                finish(i - LAG)
+        for i in range(max(0, steps - LAG), steps):
+            finish(i)
+
+        for i in range(steps):
+            first(i, 1).wait_send()
+            first(i, 0).wait_send()
+            second(i).wait_send()
+        for i in range(1, n_blk):
+            peer = (b + i) % n_blk
+            places(peer, b).wait_send()
+            places(peer, peer).wait_recv()
+            third(peer).wait_send()
+            third_in(peer).wait_recv()
+        own_pos.wait()
+        own_out.wait()
+
+    vmem = pl.BlockSpec(memory_space=pltpu.VMEM)
+    dma = pltpu.SemaphoreType.DMA
+    block = (own_rows, size, size)
+    return pl.pallas_call(
+        kernel,
+        out_shape=(
+            jax.ShapeDtypeStruct(block, jnp.float32),
+            jax.ShapeDtypeStruct(pos.shape, jnp.int32),
+        ),
+        in_specs=[vmem, vmem],
+        out_specs=(vmem, vmem),
+        scratch_shapes=[
+            pltpu.VMEM((2,) + block, jnp.float32),
+            pltpu.VMEM(block, jnp.float32),
+            pltpu.VMEM(block, jnp.float32),
+            pltpu.VMEM(block, jnp.float32),
+            dma((2, steps)), dma((2, steps)),
+            dma((steps,)), dma((steps,)),
+            dma((n_blk,)), dma((n_blk,)),
+            dma((n_blk,)), dma((n_blk,)),
+            dma((2,)),
+        ],
+        compiler_params=pltpu.CompilerParams(
+            collective_id=0, has_side_effects=True, vmem_limit_bytes=40 << 20
+        ),
+    )(partial, pos)
+
+
+def arrange(blocks, target):
+    n = blocks.shape[0]
+
+    def kernel(target_ref, src, dst, sem):
+        @pl.loop(0, n)
+        def _(r):
+            pltpu.make_async_copy(src.at[r], dst.at[target_ref[r]], sem).start()
+
+        pltpu.make_async_copy(src, dst, sem).wait()
+
+    hbm = pl.BlockSpec(memory_space=pl.ANY)
+    return pl.pallas_call(
+        kernel,
+        out_shape=jax.ShapeDtypeStruct(blocks.shape, blocks.dtype),
+        in_specs=[pl.BlockSpec(memory_space=pltpu.SMEM), hbm],
+        out_specs=hbm,
+        scratch_shapes=[pltpu.SemaphoreType.DMA],
+    )(target, blocks)
+
+
 def on_device(integrals, densities, entry_block, entry_state, entry_slot, counts, owner):
-    size = integrals.shape[1]
     hb_rows = owner.shape[0]
     n_tgt = lax.axis_size("tgt")
     n_blk = lax.axis_size("blk")
     own_rows = hb_rows // n_tgt
+    per = own_rows // n_blk
     piece = lax.all_gather(densities, "tgt", axis=0, tiled=True)
     keys, n_steps, st_bits, blk_bits = make_keys(
         entry_block, entry_state, entry_slot, jnp.sum(counts[0]), hb_rows,
@@ -104,12 +277,12 @@
     )
     place = jnp.sum((owner[None, :] < owner[:, None]).astype(jnp.int32), axis=1)
     partial = accumulate(n_steps, keys, place, integrals, piece, st_bits, blk_bits, hb_rows)
-    mine = lax.psum_scatter(partial, "tgt", scatter_dimension=0, tiled=True)
-    sorted_owner = lax.sort(owner)
-    pos = lax.dynamic_slice_in_dim(sorted_owner, lax.axis_index("tgt") * own_rows, own_rows)
-    got = lax.all_to_all(mine, "blk", split_axis=0, concat_axis=0, tiled=True)
-    got_pos = lax.all_to_all(pos, "blk", split_axis=0, concat_axis=0, tiled=True)
-    return got[jnp.argsort(got_pos)]
+    ranks = lax.axis_index("tgt") * own_rows + jnp.arange(own_rows, dtype=jnp.int32)
+    hit = (place[None, :] == ranks[:, None]).astype(jnp.int32)
+    local = jnp.sum(hit * (owner % own_rows)[None, :], axis=1).reshape(n_blk, 1, per)
+    pos = jnp.pad(local, ((0, 0), (0, 7), (0, 128 - per)))
+    got, got_pos = exchange(partial, pos, own_rows, n_blk)
+    return arrange(got, got_pos[:, 0, :per].reshape(own_rows))
 
 
 def solution(mesh):

time: 239 us -> 237 us (level)
  Pallas kernels: 19.9 us -> 193 us
  waiting for transfers between devices: 112 us -> 8.96 us
  blocking collectives: 55.5 us -> 0 us
  starting transfers between devices: 5.5 us -> 0.01 us
  local copies, waits for them, and re-layouts: 8.77 us -> 4.25 us
  other arithmetic: 19.3 us -> 15.4 us
    pallas_call x0 -> x2, Pallas kernels: none -> 174 us  [the longest x1 109 us: exchange(): pl.pallas_call(kernel, out_shape=(jax.ShapeDtypeStruct(block, jnp.float32...]
    reduce_scatter x1 -> x0, waiting for transfers between devices: 59.5 us -> none  [on_device(): mine = lax.psum_scatter(partial, 'tgt', scatter_dimension=0, tiled=True)]
    all_to_all x1 -> x0, blocking collectives: 55.5 us -> none  [on_device(): lax.all_to_all(pos, 'blk', split_axis=0, concat_axis=0, tiled=True)]
    all_to_all x1 -> x0, waiting for transfers between devices: 42.8 us -> none  [on_device(): got = lax.all_to_all(mine, 'blk', split_axis=0, concat_axis=0, tiled=True)]
    all_to_all x1 -> x0, starting transfers between devices: 5.46 us -> none  [on_device(): got = lax.all_to_all(mine, 'blk', split_axis=0, concat_axis=0, tiled=True)]
    sort x2 -> x0, other arithmetic: 4.14 us -> none  [the longest x1 2.53 us: on_device(): sorted_owner = lax.sort(owner)]
    unnamed x6 -> x4, local copies, waits for them, and re-layouts: 5.37 us -> 2.89 us
  transfers between devices with their start and end apart: 3 -> 1, of which waited for: 3 -> 1; matrix products, arithmetic and copies ran while one was open for 9% -> 7% of each run, Pallas kernels for 0% -> 0%
where the time goes in v1:
time: 237 us; the launch traced here: 236 us
  Pallas kernels  193 us (81%)
  other arithmetic  15.4 us (6%)
  between operations  14.2 us (6%)
  waiting for transfers between devices  8.96 us (4%)
  local copies, waits for them, and re-layouts  4.25 us (2%)
    pallas_call x1, Pallas kernels, exchange(): pl.pallas_call(kernel, out_shape=(jax.ShapeDtypeStruct(block, jnp.float32...  109 us
    pallas_call x1, Pallas kernels, arrange(): pl.pallas_call(kernel, out_shape=jax.ShapeDtypeStruct(blocks.shape, block...  65.3 us
    pallas_call x1, Pallas kernels, accumulate(): pl.pallas_call(kernel, out_shape=jax.ShapeDtypeStruct((hb_rows, size, siz...  19 us
    all_gather x1, waiting for transfers between devices, on_device(): piece = lax.all_gather(densities, 'tgt', axis=0, tiled=True)  8.25 us
    sort x1, other arithmetic, make_keys(): keys = lax.sort(jnp.concatenate([key, fill, tail]))  5.76 us
  transfers between devices with their start and end apart: 1, of which 1 were waited for; matrix products, arithmetic and copies ran while one was open for 7% of the time, Pallas kernels for 0%

profile of v1, /device:TPU:11, one launch (start us, length us, event | category | flops | bytes accessed | tf_op | source)
XLA Modules:
  0.0 235.7 jit_solution(1290485168660811112)
XLA Ops:
  6.5 0.0 all-gather.2.cloned.1.call-start
  6.5 0.7 all-gather.2.cloned.1.call-update
  7.3 1.3 reduce_sum.45
  8.6 0.7 iota_compare_fusion.1
  9.2 2.6 %convert_reduce_fusion = s32[128]{0:T(128)S(1)} fusion(s32[2048]{0:T(1024)} %param.11, pred[2048]{0:T(1024)(128)(4,1)S(1)} %iota_compare_fusion.1), kind=kLoop, calls=%fused_computation | loop fusion | flops 1048448 | bytes 10752 | tf_op jit(solution)/shard_map/reduce_sum | solution.py:74
  11.8 0.7 add_reduce_fusion
  13.2 0.6 slice.6
  13.8 0.9 convert_reduce_fusion.1.place_ref
  14.7 0.7 and_select_fusion
  15.4 0.2 select_reduce_fusion
  15.6 0.1 reshape.45
  15.7 0.6 select_bitcast_fusion
  16.3 2.0 add_select_fusion
  18.3 5.8 %sort.10 = (s32[2432]{0:T(1024)S(1)}, s32[2432]{0:T(1024)}) sort(s32[2432]{0:T(1024)S(1)} %pad_add_fusion, s32[2432]{0:T(1024)S(1)} %iota.29), dimensions={0}, to_apply=%region_3.4 | sort | flops 29184 | bytes 38912 | tf_op jit(solution)/shard_map/sort | solution.py:87
  24.1 8.3 %all-gather.2.cloned.1.call-done.den_hbm = bf16[60,128,128]{2,1,0:T(8,128)(2,1)} async-done(((bf16[15,128,128]{2,1,0:T(8,128)(2,1)}), bf16[60,128,128]{2,1,0:T(8,128)(2,1)}) %all-gather.2.cloned.1.call-update) | async-done | bytes 1966096 | tf_op jit(solution)/shard_map/all_gather | solution.py:273
  32.4 0.0 copy-start.1
  32.4 1.5 copy-done.1
  33.9 19.0 %shard_map.73.part = f32[128,128,128]{2,1,0:T(8,128)S(1)} custom-call(s32[1]{0:T(128)} %bitcast.n_ref, s32[2432]{0:T(1024)S(1)} %get-tuple-element.9.keys_ref, s32[128]{0:T(128)S(1)} %convert_reduce_fusion.1.place_ref, bf16[256,128,128]{2,1,0:T(8,128)(2,1)} %int_hbm.1, bf16[60,128,128]{2,1,0:T(8,128)(2,1)S(1)} %copy-done.1), custom_call_target="tpu_custom_call" | custom-call | tf_op jit(solution)/shard_map/pallas_call | solution.py:54
  53.0 108.6 %shard_map.74 = (f32[32,128,128]{2,1,0:T(8,128)S(1)}, s32[8,8,128]{2,1,0:T(8,128)S(1)}) custom-call(f32[128,128,128]{2,1,0:T(8,128)S(1)} %shard_map.73.part, s32[8,8,128]{2,1,0:T(8,128)S(1)} %pad.4.pos_ref), custom_call_target="tpu_custom_call" | custom-call | tf_op jit(solution)/shard_map/pallas_call | solution.py:222
  161.6 0.0 copy-start
  161.6 1.3 copy-done
  162.9 0.6 reshape_squeeze.3.target_ref
  163.5 65.3 %shard_map.75 = f32[32,128,128]{2,1,0:T(8,128)} custom-call(s32[32]{0:T(128)} %reshape_squeeze.3.target_ref, f32[32,128,128]{2,1,0:T(8,128)} %copy-done), custom_call_target="tpu_custom_call" | custom-call | tf_op jit(solution)/shard_map/pallas_call | solution.py:258
  (5 shorter events, 0.0 us)
Async XLA Ops:
  6.5 25.8 %all-gather.2.cloned.1.call-start = ((), (), s32[]{:S(2)}) async-start(), calls=%async_computation | async-start | bytes 2457600 | tf_op jit(solution)/shard_map/all_gather | solution.py:273
  32.4 1.5 copy-start.1
  161.6 1.4 copy-start
Sparse Core Ops, SparseCore 0:
  8.9 23.3 all-gather.1

commit v2 on v1

--- a/solution.py
+++ b/solution.py
@@ -258,7 +258,7 @@
     return pl.pallas_call(
         kernel,
         out_shape=jax.ShapeDtypeStruct(blocks.shape, blocks.dtype),
-        in_specs=[pl.BlockSpec(memory_space=pltpu.SMEM), hbm],
+        in_specs=[pl.BlockSpec(memory_space=pltpu.SMEM), pl.BlockSpec(memory_space=pltpu.VMEM)],
         out_specs=hbm,
         scratch_shapes=[pltpu.SemaphoreType.DMA],
     )(target, blocks)

time: 237 us -> 177 us (0.75)
  Pallas kernels: 193 us -> 133 us
    pallas_call x1, Pallas kernels: 65.3 us -> 2.89 us  [arrange(): pl.pallas_call(kernel, out_shape=jax.ShapeDtypeStruct(blocks.shape, block...]
    pallas_call x1, Pallas kernels: 19 us -> 29.6 us  [accumulate(): pl.pallas_call(kernel, out_shape=jax.ShapeDtypeStruct((hb_rows, size, siz...]
    pallas_call x1, Pallas kernels: 109 us -> 100 us  [exchange(): pl.pallas_call(kernel, out_shape=(jax.ShapeDtypeStruct(block, jnp.float32...]
  transfers between devices with their start and end apart: 1 -> 1, of which waited for: 1 -> 1; matrix products, arithmetic and copies ran while one was open for 7% -> 9% of each run, Pallas kernels for 0% -> 0%
where the time goes in v2:
time: 177 us; the launch traced here: 176 us
  Pallas kernels  133 us (75%)
  other arithmetic  15.4 us (9%)
  between operations  14.2 us (8%)
  waiting for transfers between devices  8.96 us (5%)
  local copies, waits for them, and re-layouts  4.25 us (2%)
    pallas_call x1, Pallas kernels, exchange(): pl.pallas_call(kernel, out_shape=(jax.ShapeDtypeStruct(block, jnp.float32...  100 us
    pallas_call x1, Pallas kernels, accumulate(): pl.pallas_call(kernel, out_shape=jax.ShapeDtypeStruct((hb_rows, size, siz...  29.6 us
    all_gather x1, waiting for transfers between devices, on_device(): piece = lax.all_gather(densities, 'tgt', axis=0, tiled=True)  8.25 us
    sort x1, other arithmetic, make_keys(): keys = lax.sort(jnp.concatenate([key, fill, tail]))  5.76 us
  transfers between devices with their start and end apart: 1, of which 1 were waited for; matrix products, arithmetic and copies ran while one was open for 9% of the time, Pallas kernels for 0%

profile of v2, /device:TPU:11, one launch (start us, length us, event | category | flops | bytes accessed | tf_op | source)
XLA Modules:
  0.0 175.7 jit_solution(15421754798351943185)
XLA Ops:
  6.5 0.0 all-gather.2.cloned.1.call-start
  6.5 0.7 all-gather.2.cloned.1.call-update
  7.3 1.3 reduce_sum.45
  8.6 0.7 iota_compare_fusion.1
  9.2 2.6 %convert_reduce_fusion = s32[128]{0:T(128)S(1)} fusion(s32[2048]{0:T(1024)} %param.11, pred[2048]{0:T(1024)(128)(4,1)S(1)} %iota_compare_fusion.1), kind=kLoop, calls=%fused_computation | loop fusion | flops 1048448 | bytes 10752 | tf_op jit(solution)/shard_map/reduce_sum | solution.py:74
  11.8 0.7 add_reduce_fusion
  13.2 0.6 slice.6
  13.8 0.9 convert_reduce_fusion.1.place_ref
  14.7 0.7 and_select_fusion
  15.4 0.2 select_reduce_fusion
  15.6 0.1 reshape.45
  15.7 0.6 select_bitcast_fusion
  16.3 2.0 %add_select_fusion = s32[2048]{0:T(1024)S(1)} fusion(s32[2048]{0:T(1024)} %param.10, s32[2048]{0:T(1024)} %param.9, s32[2048]{0:T(1024)} %param.11, s32[]{:T(128)} %bitcast.1, s32[]{:T(128)} %reduce_sum.45), kind=kLoop, calls=%fused_computation.6 | loop fusion | flops 12288 | bytes 32776 | tf_op jit(solution)/shard_map/jit(_where)/select_n | solution.py:81
  18.3 5.8 %sort.10 = (s32[2432]{0:T(1024)S(1)}, s32[2432]{0:T(1024)}) sort(s32[2432]{0:T(1024)S(1)} %pad_add_fusion, s32[2432]{0:T(1024)S(1)} %iota.29), dimensions={0}, to_apply=%region_3.4 | sort | flops 29184 | bytes 38912 | tf_op jit(solution)/shard_map/sort | solution.py:87
  24.1 8.3 %all-gather.2.cloned.1.call-done.den_hbm = bf16[60,128,128]{2,1,0:T(8,128)(2,1)} async-done(((bf16[15,128,128]{2,1,0:T(8,128)(2,1)}), bf16[60,128,128]{2,1,0:T(8,128)(2,1)}) %all-gather.2.cloned.1.call-update) | async-done | bytes 1966096 | tf_op jit(solution)/shard_map/all_gather | solution.py:273
  32.4 0.0 copy-start.1
  32.4 1.5 copy-done.1
  33.9 29.6 %shard_map.73.part = f32[128,128,128]{2,1,0:T(8,128)S(1)} custom-call(s32[1]{0:T(128)} %bitcast.n_ref, s32[2432]{0:T(1024)S(1)} %get-tuple-element.9.keys_ref, s32[128]{0:T(128)S(1)} %convert_reduce_fusion.1.place_ref, bf16[256,128,128]{2,1,0:T(8,128)(2,1)} %int_hbm.1, bf16[60,128,128]{2,1,0:T(8,128)(2,1)S(1)} %copy-done.1), custom_call_target="tpu_custom_call" | custom-call | tf_op jit(solution)/shard_map/pallas_call | solution.py:54
  63.5 100.4 %shard_map.74 = (f32[32,128,128]{2,1,0:T(8,128)S(1)}, s32[8,8,128]{2,1,0:T(8,128)S(1)}) custom-call(f32[128,128,128]{2,1,0:T(8,128)S(1)} %shard_map.73.part, s32[8,8,128]{2,1,0:T(8,128)S(1)} %pad.4.pos_ref), custom_call_target="tpu_custom_call" | custom-call | tf_op jit(solution)/shard_map/pallas_call | solution.py:222
  163.9 0.0 copy-start
  163.9 1.3 copy-done
  165.3 0.6 reshape_squeeze.3.target_ref
  165.9 2.9 %shard_map.75 = f32[32,128,128]{2,1,0:T(8,128)} custom-call(s32[32]{0:T(128)} %reshape_squeeze.3.target_ref, f32[32,128,128]{2,1,0:T(8,128)} %copy-done), custom_call_target="tpu_custom_call" | custom-call | tf_op jit(solution)/shard_map/pallas_call | solution.py:258
  (5 shorter events, 0.0 us)
Async XLA Ops:
  6.5 25.8 %all-gather.2.cloned.1.call-start = ((), (), s32[]{:S(2)}) async-start(), calls=%async_computation | async-start | bytes 2457600 | tf_op jit(solution)/shard_map/all_gather | solution.py:273
  32.4 1.5 copy-start.1
  163.9 1.4 copy-start
Sparse Core Ops, SparseCore 0:
  8.9 23.3 all-gather.1

commit v3 on v2

--- a/solution.py
+++ b/solution.py
@@ -6,7 +6,7 @@
 from jax.sharding import PartitionSpec as P
 
 CHUNK = 4
-UNROLL = 2
+UNROLL = 4
 STEPS = 8
 LAG = 1
 MESH = pl.DeviceIdType.MESH
@@ -89,6 +89,19 @@
     return keys, n_steps.reshape(1), st_bits, blk_bits
 
 
+LEVELS = 32767.0
+SMALLEST = 1e-33
+
+
+def narrow(x):
+    top = jnp.maximum(jnp.max(jnp.abs(x), axis=0, keepdims=True), SMALLEST)
+    return jnp.round(x * (LEVELS / top)).astype(jnp.int32).astype(jnp.int16), top * (1.0 / LEVELS)
+
+
+def widen(q, step):
+    return q.astype(jnp.int32).astype(jnp.float32) * step
+
+
 def exchange(partial, pos, own_rows, n_blk):
     size = partial.shape[-1]
     steps = min(STEPS, n_blk)
@@ -96,8 +109,9 @@
     dests = n_blk // steps
     per = own_rows // n_blk
 
-    def kernel(part, pos_ref, out, pos_out, r1, s2, r2, mine,
-               s1_send, s1_recv, s2_send, s2_recv, s3_send, s3_recv, p_send, p_recv, own_sem):
+    def kernel(part, pos_ref, out, step_out, r1, s2, r2, s3, step2, step2_in, step3,
+               s1_send, s1_recv, s2_send, s2_recv, t2_send, t2_recv, s3_send, s3_recv,
+               t3_send, t3_recv, own_sem):
         t = lax.axis_index("tgt")
         b = lax.axis_index("blk")
         y, c = t // 2, t % 2
@@ -136,68 +150,82 @@
                 device_id_type=MESH,
             )
 
-        def third(dest):
-            return pltpu.make_async_remote_copy(
-                src_ref=mine.at[pl.ds(dest * per, per)],
-                dst_ref=out.at[pl.ds(b * per, per)],
+        def second_steps(i):
+            return pltpu.make_async_remote_copy(
+                src_ref=step2.at[i],
+                dst_ref=step2_in.at[i],
+                send_sem=t2_send.at[i],
+                recv_sem=t2_recv.at[i],
+                device_id={"tgt": across},
+                device_id_type=MESH,
+            )
+
+        def third(dest, slot):
+            return pltpu.make_async_remote_copy(
+                src_ref=s3.at[pl.ds(dest * per, per)],
+                dst_ref=out.at[pl.ds(slot * per, per)],
                 send_sem=s3_send.at[dest],
-                recv_sem=s3_recv.at[b],
+                recv_sem=s3_recv.at[slot],
                 device_id={"blk": dest},
                 device_id_type=MESH,
             )
 
-        def third_in(src):
-            return pltpu.make_async_remote_copy(
-                src_ref=mine.at[pl.ds(src * per, per)],
-                dst_ref=out.at[pl.ds(src * per, per)],
-                send_sem=s3_send.at[src],
-                recv_sem=s3_recv.at[src],
-                device_id={"blk": src},
-                device_id_type=MESH,
-            )
-
-        def places(dest, slot):
-            return pltpu.make_async_remote_copy(
-                src_ref=pos_ref.at[dest],
-                dst_ref=pos_out.at[slot],
-                send_sem=p_send.at[dest],
-                recv_sem=p_recv.at[slot],
+        def third_steps(dest, slot):
+            return pltpu.make_async_remote_copy(
+                src_ref=step3.at[dest],
+                dst_ref=step_out.at[slot],
+                send_sem=t3_send.at[dest],
+                recv_sem=t3_recv.at[slot],
                 device_id={"blk": dest},
                 device_id_type=MESH,
             )
 
         own_out = pltpu.make_async_copy(
-            mine.at[pl.ds(b * per, per)], out.at[pl.ds(b * per, per)], own_sem.at[0]
+            s3.at[pl.ds(b * per, per)], out.at[pl.ds(b * per, per)], own_sem.at[0]
         )
-        own_pos = pltpu.make_async_copy(pos_ref.at[b], pos_out.at[b], own_sem.at[1])
+        own_steps = pltpu.make_async_copy(step3.at[b], step_out.at[b], own_sem.at[1])
 
         for i in range(steps):
             first(i, 1).start()
             first(i, 0).start()
-        own_pos.start()
-        for i in range(1, n_blk):
-            places((b + i) % n_blk, b).start()
-
-        def dest_of(i, j):
-            return ((b // dests + 1 + i) % steps) * dests + (b % dests + j) % dests
 
         def finish(i):
+            first(i, 0).wait_recv()
             second(i).wait_recv()
-            at = pl.ds(span(i), rows)
-            mine[at] = mine[at] + r2[at]
+            second_steps(i).wait_recv()
+            steps_in = step2_in[i]
             for j in range(dests):
+                dest = ((b // dests + 1 + i) % steps) * dests + (b % dests + j) % dests
+                step3[dest] = pos_ref[dest]
+                for k in range(per):
+                    row = dest * per + k
+                    at = ((b % dests + j) % dests) * per + k if dests > 1 else k
+                    if dests > 1:
+                        scale = step2_in[i, pl.ds(at, 1), :]
+                    else:
+                        scale = steps_in[k:k + 1]
+                    total = part[(y * 2 + c) * own_rows + row] + r1[0, row] + widen(r2[row], scale)
+                    q, step = narrow(total)
+                    s3[row] = q
+                    step3[dest, k:k + 1, :] = step
                 if i == steps - 1 and j == 0:
                     own_out.start()
+                    own_steps.start()
                 else:
-                    third(dest_of(i, j)).start()
+                    third(dest, b).start()
+                    third_steps(dest, b).start()
 
         for i in range(steps):
-            at = pl.ds(span(i), rows)
             first(i, 1).wait_recv()
-            s2[at] = part[pl.ds(((1 - y) * 2 + c) * own_rows + span(i), rows)] + r1[1, at]
+            for k in range(rows):
+                row = span(i) + k
+                q, step = narrow(part[((1 - y) * 2 + c) * own_rows + row] + r1[1, row])
+                s2[row] = q
+                step2[i, k:k + 1, :] = step
+            for k in range(rows, 8):
+                step2[i, k:k + 1, :] = jnp.zeros((1, size), jnp.float32)
             second(i).start()
-            first(i, 0).wait_recv()
-            mine[at] = part[pl.ds((y * 2 + c) * own_rows + span(i), rows)] + r1[0, at]
+            second_steps(i).start()
             if i >= LAG:
                 finish(i - LAG)
         for i in range(max(0, steps - LAG), steps):
@@ -207,13 +235,14 @@
             first(i, 1).wait_send()
             first(i, 0).wait_send()
             second(i).wait_send()
+            second_steps(i).wait_send()
         for i in range(1, n_blk):
             peer = (b + i) % n_blk
-            places(peer, b).wait_send()
-            places(peer, peer).wait_recv()
-            third(peer).wait_send()
-            third_in(peer).wait_recv()
-        own_pos.wait()
+            third(peer, b).wait_send()
+            third_steps(peer, b).wait_send()
+            third(peer, peer).wait_recv()
+            third_steps(peer, peer).wait_recv()
+        own_steps.wait()
         own_out.wait()
 
     vmem = pl.BlockSpec(memory_space=pltpu.VMEM)
@@ -222,17 +251,21 @@
     return pl.pallas_call(
         kernel,
         out_shape=(
-            jax.ShapeDtypeStruct(block, jnp.float32),
-            jax.ShapeDtypeStruct(pos.shape, jnp.int32),
+            jax.ShapeDtypeStruct(block, jnp.int16),
+            jax.ShapeDtypeStruct(pos.shape, jnp.float32),
         ),
         in_specs=[vmem, vmem],
         out_specs=(vmem, vmem),
         scratch_shapes=[
             pltpu.VMEM((2,) + block, jnp.float32),
-            pltpu.VMEM(block, jnp.float32),
-            pltpu.VMEM(block, jnp.float32),
-            pltpu.VMEM(block, jnp.float32),
+            pltpu.VMEM(block, jnp.int16),
+            pltpu.VMEM(block, jnp.int16),
+            pltpu.VMEM(block, jnp.int16),
+            pltpu.VMEM((steps, 8, size), jnp.float32),
+            pltpu.VMEM((steps, 8, size), jnp.float32),
+            pltpu.VMEM((n_blk, 8, size), jnp.float32),
             dma((2, steps)), dma((2, steps)),
+            dma((steps,)), dma((steps,)),
             dma((steps,)), dma((steps,)),
             dma((n_blk,)), dma((n_blk,)),
             dma((n_blk,)), dma((n_blk,)),
@@ -244,24 +277,29 @@
     )(partial, pos)
 
 
-def arrange(blocks, target):
-    n = blocks.shape[0]
-
-    def kernel(target_ref, src, dst, sem):
-        @pl.loop(0, n)
-        def _(r):
-            pltpu.make_async_copy(src.at[r], dst.at[target_ref[r]], sem).start()
-
-        pltpu.make_async_copy(src, dst, sem).wait()
-
-    hbm = pl.BlockSpec(memory_space=pl.ANY)
+def arrange(blocks, sizes, target):
+    n, size, _ = blocks.shape
+    n_blk = sizes.shape[0]
+    per = n // n_blk
+
+    def kernel(target_ref, src, sizes_ref, dst, wide, sem):
+        @pl.loop(0, n_blk)
+        def _(s):
+            for k in range(per):
+                r = s * per + k
+                wide[r] = widen(src[r], sizes_ref[s, k:k + 1, :])
+                pltpu.make_async_copy(wide.at[r], dst.at[target_ref[r]], sem).start()
+
+        pltpu.make_async_copy(wide, dst, sem).wait()
+
+    vmem = pl.BlockSpec(memory_space=pltpu.VMEM)
     return pl.pallas_call(
         kernel,
-        out_shape=jax.ShapeDtypeStruct(blocks.shape, blocks.dtype),
-        in_specs=[pl.BlockSpec(memory_space=pltpu.SMEM), pl.BlockSpec(memory_space=pltpu.VMEM)],
-        out_specs=hbm,
-        scratch_shapes=[pltpu.SemaphoreType.DMA],
-    )(target, blocks)
+        out_shape=jax.ShapeDtypeStruct(blocks.shape, jnp.float32),
+        in_specs=[pl.BlockSpec(memory_space=pltpu.SMEM), vmem, vmem],
+        out_specs=pl.BlockSpec(memory_space=pl.ANY),
+        scratch_shapes=[pltpu.VMEM(blocks.shape, jnp.float32), pltpu.SemaphoreType.DMA],
+    )(target, blocks, sizes)
 
 
 def on_device(integrals, densities, entry_block, entry_state, entry_slot, counts, owner):
@@ -280,9 +318,9 @@
     ranks = lax.axis_index("tgt") * own_rows + jnp.arange(own_rows, dtype=jnp.int32)
     hit = (place[None, :] == ranks[:, None]).astype(jnp.int32)
     local = jnp.sum(hit * (owner % own_rows)[None, :], axis=1).reshape(n_blk, 1, per)
-    pos = jnp.pad(local, ((0, 0), (0, 7), (0, 128 - per)))
-    got, got_pos = exchange(partial, pos, own_rows, n_blk)
-    return arrange(got, got_pos[:, 0, :per].reshape(own_rows))
+    pos = jnp.pad(local, ((0, 0), (7, 0), (0, integrals.shape[1] - per))).astype(jnp.float32)
+    got, sizes = exchange(partial, pos, own_rows, n_blk)
+    return arrange(got, sizes, sizes[:, 7, :per].astype(jnp.int32).reshape(own_rows))
 
 
 def solution(mesh):

time: 177 us -> 127 us (0.72)
  Pallas kernels: 133 us -> 84.6 us
    pallas_call x2, Pallas kernels: 103 us -> 58.5 us  [the longest x1 56 us: exchange(): pl.pallas_call(kernel, out_shape=(jax.ShapeDtypeStruct(block, jnp.int16),...]
    pallas_call x1, Pallas kernels: 29.6 us -> 26.1 us  [accumulate(): pl.pallas_call(kernel, out_shape=jax.ShapeDtypeStruct((hb_rows, size, siz...]
  transfers between devices with their start and end apart: 1 -> 1, of which waited for: 1 -> 1; matrix products, arithmetic and copies ran while one was open for 9% -> 13% of each run, Pallas kernels for 0% -> 0%
where the time goes in v3:
time: 127 us
  Pallas kernels  84.6 us (67%)
  other arithmetic  15.4 us (12%)
  between operations  14.1 us (11%)
  waiting for transfers between devices  8.98 us (7%)
  local copies, waits for them, and re-layouts  3.89 us (3%)
    pallas_call x1, Pallas kernels, exchange(): pl.pallas_call(kernel, out_shape=(jax.ShapeDtypeStruct(block, jnp.int16),...  56 us
    pallas_call x1, Pallas kernels, accumulate(): pl.pallas_call(kernel, out_shape=jax.ShapeDtypeStruct((hb_rows, size, siz...  26.1 us
    all_gather x1, waiting for transfers between devices, on_device(): piece = lax.all_gather(densities, 'tgt', axis=0, tiled=True)  8.27 us
    sort x1, other arithmetic, make_keys(): keys = lax.sort(jnp.concatenate([key, fill, tail]))  5.76 us
    reduce_sum x1, other arithmetic, make_keys(): jnp.sum(((entry_slot[:, None] == slots[None, :]) & valid[:, None]).astype...  2.62 us
  transfers between devices with their start and end apart: 1, of which 1 were waited for; matrix products, arithmetic and copies ran while one was open for 13% of the time, Pallas kernels for 0%

profile of v3, /device:TPU:11, one launch (start us, length us, event | category | flops | bytes accessed | tf_op | source)
XLA Modules:
  0.0 127.0 jit_solution(16363535516392667360)
XLA Ops:
  6.5 0.0 all-gather.2.cloned.1.call-start
  6.5 0.7 all-gather.2.cloned.1.call-update
  7.3 1.3 %reduce_sum.45 = s32[]{:T(128)} reduce(s32[1,4]{1,0:T(1,128)} %param.12, s32[]{:T(128)} %constant.49.clone.1), dimensions={0,1}, to_apply=%region_0.0 | reduce | flops 3 | bytes 24 | tf_op jit(solution)/shard_map/reduce_sum | solution.py:313
  8.6 0.7 iota_compare_fusion.1
  9.2 2.6 %convert_reduce_fusion = s32[128]{0:T(128)S(1)} fusion(s32[2048]{0:T(1024)} %param.11, pred[2048]{0:T(1024)(128)(4,1)S(1)} %iota_compare_fusion.1), kind=kLoop, calls=%fused_computation | loop fusion | flops 1048448 | bytes 10752 | tf_op jit(solution)/shard_map/reduce_sum | solution.py:74
  11.8 0.7 add_reduce_fusion
  13.2 0.6 slice.6
  13.8 0.9 convert_reduce_fusion.1.place_ref
  14.7 0.7 and_select_fusion
  15.4 0.2 select_reduce_fusion
  15.6 0.1 reshape.48
  15.6 0.6 select_bitcast_fusion
  16.3 2.0 %add_select_fusion = s32[2048]{0:T(1024)S(1)} fusion(s32[2048]{0:T(1024)} %param.10, s32[2048]{0:T(1024)} %param.9, s32[2048]{0:T(1024)} %param.11, s32[]{:T(128)} %bitcast.1, s32[]{:T(128)} %reduce_sum.45), kind=kLoop, calls=%fused_computation.7 | loop fusion | flops 12288 | bytes 32776 | tf_op jit(solution)/shard_map/jit(_where)/select_n | solution.py:81
  18.3 5.8 %sort.10 = (s32[2432]{0:T(1024)S(1)}, s32[2432]{0:T(1024)}) sort(s32[2432]{0:T(1024)S(1)} %pad_add_fusion, s32[2432]{0:T(1024)S(1)} %iota.29), dimensions={0}, to_apply=%region_3.4 | sort | flops 29184 | bytes 38912 | tf_op jit(solution)/shard_map/sort | solution.py:87
  24.1 8.3 %all-gather.2.cloned.1.call-done.den_hbm = bf16[60,128,128]{2,1,0:T(8,128)(2,1)} async-done(((bf16[15,128,128]{2,1,0:T(8,128)(2,1)}), bf16[60,128,128]{2,1,0:T(8,128)(2,1)}) %all-gather.2.cloned.1.call-update) | async-done | bytes 1966096 | tf_op jit(solution)/shard_map/all_gather | solution.py:311
  32.4 0.0 copy-start
  32.4 1.5 %copy-done = bf16[60,128,128]{2,1,0:T(8,128)(2,1)S(1)} copy-done((bf16[60,128,128]{2,1,0:T(8,128)(2,1)S(1)}, bf16[60,128,128]{2,1,0:T(8,128)(2,1)}, u32[]{:S(2)}) %copy-start) | copy-done | bytes 1966104
  33.9 26.1 %shard_map.73.part = f32[128,128,128]{2,1,0:T(8,128)S(1)} custom-call(s32[1]{0:T(128)} %bitcast.n_ref, s32[2432]{0:T(1024)S(1)} %get-tuple-element.9.keys_ref, s32[128]{0:T(128)S(1)} %convert_reduce_fusion.1.place_ref, bf16[256,128,128]{2,1,0:T(8,128)(2,1)} %int_hbm.1, bf16[60,128,128]{2,1,0:T(8,128)(2,1)S(1)} %copy-done), custom_call_target="tpu_custom_call" | custom-call | tf_op jit(solution)/shard_map/pallas_call | solution.py:54
  60.0 56.0 %shard_map.74 = (s16[32,128,128]{2,1,0:T(8,128)(2,1)S(1)}, f32[8,8,128]{2,1,0:T(8,128)S(1)}) custom-call(f32[128,128,128]{2,1,0:T(8,128)S(1)} %shard_map.73.part, f32[8,8,128]{2,1,0:T(8,128)S(1)} %pad_convert_fusion.pos_ref), custom_call_target="tpu_custom_call" | custom-call | tf_op jit(solution)/shard_map/pallas_call | solution.py:251
  116.0 0.0 copy-start.1
  116.0 1.0 copy-done.1
  117.0 0.6 convert_element_type.21.target_ref
  117.6 0.0 copy-done.2
  117.6 2.5 %shard_map.75 = f32[32,128,128]{2,1,0:T(8,128)} custom-call(s32[32]{0:T(128)} %convert_element_type.21.target_ref, s16[32,128,128]{2,1,0:T(8,128)(2,1)} %copy-done.1, f32[8,8,128]{2,1,0:T(8,128)} %copy-done.2), custom_call_target="tpu_custom_call" | custom-call | tf_op jit(solution)/shard_map/pallas_call | solution.py:296
  (6 shorter events, 0.0 us)
Async XLA Ops:
  6.5 25.8 %all-gather.2.cloned.1.call-start = ((), (), s32[]{:S(2)}) async-start(), calls=%async_computation | async-start | bytes 2457600 | tf_op jit(solution)/shard_map/all_gather | solution.py:311
  32.4 1.5 %copy-start = (bf16[60,128,128]{2,1,0:T(8,128)(2,1)S(1)}, bf16[60,128,128]{2,1,0:T(8,128)(2,1)}, u32[]{:S(2)}) copy-start(bf16[60,128,128]{2,1,0:T(8,128)(2,1)} %all-gather.2.cloned.1.call-done.den_hbm) | copy-start | bytes 5898244
  116.0 1.0 copy-start.1
  116.9 0.6 copy-start.2
Sparse Core Ops, SparseCore 0:
  8.9 23.3 all-gather.1

commit v4 on v3

--- a/solution.py
+++ b/solution.py
@@ -6,7 +6,7 @@
 from jax.sharding import PartitionSpec as P
 
 CHUNK = 4
-UNROLL = 4
+UNROLL = 8
 STEPS = 8
 LAG = 1
 MESH = pl.DeviceIdType.MESH
@@ -16,25 +16,30 @@
     return max(1, (n - 1).bit_length())
 
 
-def accumulate(n_steps, keys, place, integrals, densities, st_bits, blk_bits, hb_rows):
-    states, size, _ = densities.shape
-    held = integrals.shape[0]
+def accumulate(n_steps, keys, place, integrals, pieces, groups, st_bits, blk_bits, hb_rows):
+    s_group, size, _ = pieces[0].shape
+    states = s_group * len(pieces)
     st_mask = (1 << st_bits) - 1
     blk_mask = (1 << blk_bits) - 1
 
-    def kernel(n_ref, keys_ref, place_ref, int_hbm, den_hbm, acc, ints, dens, sems):
-        load_ints = pltpu.make_async_copy(int_hbm, ints, sems.at[0])
-        load_dens = pltpu.make_async_copy(den_hbm, dens.at[pl.ds(0, states)], sems.at[1])
-        load_ints.start()
-        load_dens.start()
+    def kernel(n_ref, keys_ref, place_ref, groups_ref, ints, *rest):
+        den_refs, (acc, dens, sems) = rest[:len(pieces)], rest[len(pieces):]
+        loads = [
+            pltpu.make_async_copy(
+                ref, dens.at[pl.ds(groups_ref[i] * s_group, s_group)], sems.at[i]
+            )
+            for i, ref in enumerate(den_refs)
+        ]
+        for load in loads:
+            load.start()
         dens[states] = jnp.zeros((size, size), dens.dtype)
 
         @pl.loop(0, hb_rows)
         def _(j):
             acc[j] = jnp.zeros((size, size), jnp.float32)
 
-        load_ints.wait()
-        load_dens.wait()
+        for load in loads:
+            load.wait()
 
         @pl.loop(0, n_ref[0])
         def _(step):
@@ -50,19 +55,19 @@
                 acc[row] += prod
 
     smem = pl.BlockSpec(memory_space=pltpu.SMEM)
+    vmem = pl.BlockSpec(memory_space=pltpu.VMEM)
     hbm = pl.BlockSpec(memory_space=pl.ANY)
     return pl.pallas_call(
         kernel,
         out_shape=jax.ShapeDtypeStruct((hb_rows, size, size), jnp.float32),
-        in_specs=[smem, smem, smem, hbm, hbm],
-        out_specs=pl.BlockSpec(memory_space=pltpu.VMEM),
+        in_specs=[smem] * 4 + [vmem] + [hbm] * len(pieces),
+        out_specs=vmem,
         scratch_shapes=[
-            pltpu.VMEM((held, size, size), integrals.dtype),
-            pltpu.VMEM((states + 1, size, size), densities.dtype),
-            pltpu.SemaphoreType.DMA((2,)),
+            pltpu.VMEM((states + 1, size, size), pieces[0].dtype),
+            pltpu.SemaphoreType.DMA((len(pieces),)),
         ],
-        compiler_params=pltpu.CompilerParams(vmem_limit_bytes=40 << 20),
-    )(n_steps, keys, place, integrals, densities)
+        compiler_params=pltpu.CompilerParams(vmem_limit_bytes=32 << 20),
+    )(n_steps, keys, place, groups, integrals, *pieces)
 
 
 def make_keys(entry_block, entry_state, entry_slot, live, hb_rows, held, states):
@@ -84,7 +89,7 @@
     total = e_cap + fill.shape[0]
     group = CHUNK * UNROLL
     tail = jnp.full(((-total) % group,), last, jnp.int32)
-    keys = lax.sort(jnp.concatenate([key, fill, tail]))
+    keys = lax.sort(jnp.concatenate([key, fill, tail]), is_stable=False)
     n_steps = (jnp.sum(per_slot + spare) + group - 1) // group
     return keys, n_steps.reshape(1), st_bits, blk_bits
 
@@ -308,14 +313,23 @@
     n_blk = lax.axis_size("blk")
     own_rows = hb_rows // n_tgt
     per = own_rows // n_blk
-    piece = lax.all_gather(densities, "tgt", axis=0, tiled=True)
+    t = lax.axis_index("tgt")
+    over = [(i, i ^ 2) for i in range(n_tgt)]
+    beside = [(i, i ^ 1) for i in range(n_tgt)]
+    far = lax.ppermute(densities, "tgt", over)
+    near = lax.ppermute(densities, "tgt", beside)
+    far_near = lax.ppermute(far, "tgt", beside)
+    pieces = (densities, near, far, far_near)
+    groups = t ^ jnp.arange(4, dtype=jnp.int32)
     keys, n_steps, st_bits, blk_bits = make_keys(
         entry_block, entry_state, entry_slot, jnp.sum(counts[0]), hb_rows,
-        integrals.shape[0], piece.shape[0],
+        integrals.shape[0], densities.shape[0] * n_tgt,
     )
     place = jnp.sum((owner[None, :] < owner[:, None]).astype(jnp.int32), axis=1)
-    partial = accumulate(n_steps, keys, place, integrals, piece, st_bits, blk_bits, hb_rows)
-    ranks = lax.axis_index("tgt") * own_rows + jnp.arange(own_rows, dtype=jnp.int32)
+    partial = accumulate(
+        n_steps, keys, place, integrals, pieces, groups, st_bits, blk_bits, hb_rows
+    )
+    ranks = t * own_rows + jnp.arange(own_rows, dtype=jnp.int32)
     hit = (place[None, :] == ranks[:, None]).astype(jnp.int32)
     local = jnp.sum(hit * (owner % own_rows)[None, :], axis=1).reshape(n_blk, 1, per)
     pos = jnp.pad(local, ((0, 0), (7, 0), (0, integrals.shape[1] - per))).astype(jnp.float32)

time: 127 us -> 101 us (0.80)
  between operations: 14.1 us -> 0.81 us
  Pallas kernels: 84.6 us -> 73.3 us
  waiting for transfers between devices: 8.98 us -> 1.06 us
  starting transfers between devices: 0.01 us -> 3.74 us
  local copies, waits for them, and re-layouts: 3.89 us -> 6.66 us
    all_gather x1 -> x0, waiting for transfers between devices: 8.27 us -> none  [on_device(): piece = lax.all_gather(densities, 'tgt', axis=0, tiled=True)]
    pallas_call x1, Pallas kernels: 26.1 us -> 19.1 us  [accumulate(): pl.pallas_call(kernel, out_shape=jax.ShapeDtypeStruct((hb_rows, size, siz...]
    pallas_call x1, Pallas kernels: 56 us -> 51.6 us  [exchange(): pl.pallas_call(kernel, out_shape=(jax.ShapeDtypeStruct(block, jnp.int16),...]
    ppermute x0 -> x3, starting transfers between devices: none -> 3.74 us  [the longest x1 1.55 us: on_device(): far_near = lax.ppermute(far, 'tgt', beside)]
    unnamed x6 -> x8, local copies, waits for them, and re-layouts: 2.53 us -> 5.39 us
  transfers between devices with their start and end apart: 1 -> 3, of which waited for: 1 -> 1; matrix products, arithmetic and copies ran while one was open for 13% -> 15% of each run, Pallas kernels for 0% -> 0%
where the time goes in v4:
time: 101 us; the launch traced here: 100 us
  Pallas kernels  73.3 us (73%)
  other arithmetic  14.5 us (14%)
  local copies, waits for them, and re-layouts  6.66 us (7%)
  starting transfers between devices  3.74 us (4%)
  waiting for transfers between devices  1.06 us (1%)
    pallas_call x1, Pallas kernels, exchange(): pl.pallas_call(kernel, out_shape=(jax.ShapeDtypeStruct(block, jnp.int16),...  51.6 us
    pallas_call x1, Pallas kernels, accumulate(): pl.pallas_call(kernel, out_shape=jax.ShapeDtypeStruct((hb_rows, size, siz...  19.1 us
    unnamed x8, local copies, waits for them, and re-layouts  5.39 us
    sort x1, other arithmetic, make_keys(): keys = lax.sort(jnp.concatenate([key, fill, tail]), is_stable=False)  4.9 us
    reduce_sum x1, other arithmetic, make_keys(): jnp.sum(((entry_slot[:, None] == slots[None, :]) & valid[:, None]).astype...  2.62 us
    pallas_call x1, Pallas kernels, arrange(): pl.pallas_call(kernel, out_shape=jax.ShapeDtypeStruct(blocks.shape, jnp.f...  2.53 us
  transfers between devices with their start and end apart: 3, of which 1 were waited for; matrix products, arithmetic and copies ran while one was open for 15% of the time, Pallas kernels for 0%

profile of v4, /device:TPU:11, one launch (start us, length us, event | category | flops | bytes accessed | tf_op | source)
XLA Modules:
  0.0 100.1 jit_solution(10960993924951920976)
XLA Ops:
  0.0 1.2 %collective-permute-start.1 = (bf16[15,128,128]{2,1,0:T(8,128)(2,1)}, bf16[15,128,128]{2,1,0:T(8,128)(2,1)S(1)}, u32[]{:S(2)}, u32[]{:S(2)}) collective-permute-start(bf16[15,128,128]{2,1,0:T(8,128)(2,1)} %rest_0_.1), channel_id=1, source_target_pairs={{0,16},{8,24},{16,0},{24,8},{1,17},{9,25},{17,1},{25,9},{2,18},{10... | collective-permute-start | bytes 1474568 | tf_op jit(solution)/shard_map/ppermute | solution.py:319
  1.2 1.0 collective-permute-start
  2.2 1.3 %reduce_sum.45 = s32[]{:T(128)} reduce(s32[1,4]{1,0:T(1,128)} %param.12, s32[]{:T(128)} %constant.48.clone.1), dimensions={0,1}, to_apply=%region_0.0 | reduce | flops 3 | bytes 24 | tf_op jit(solution)/shard_map/reduce_sum | solution.py:325
  3.5 0.7 iota_compare_fusion.1
  4.1 2.6 %convert_reduce_fusion = s32[128]{0:T(128)S(1)} fusion(s32[2048]{0:T(1024)} %param.11, pred[2048]{0:T(1024)(128)(4,1)S(1)} %iota_compare_fusion.1), kind=kLoop, calls=%fused_computation | loop fusion | flops 1048448 | bytes 10752 | tf_op jit(solution)/shard_map/reduce_sum | solution.py:79
  6.8 0.7 add_reduce_fusion
  7.5 0.6 slice.6
  8.1 1.9 %add_select_fusion = s32[2048]{0:T(1024)S(1)} fusion(s32[2048]{0:T(1024)} %param.10, s32[2048]{0:T(1024)} %param.9, s32[2048]{0:T(1024)} %param.11, s32[]{:T(128)} %bitcast.1, s32[]{:T(128)} %reduce_sum.45), kind=kLoop, calls=%fused_computation.7 | loop fusion | flops 12288 | bytes 32776 | tf_op jit(solution)/shard_map/jit(_where)/select_n | solution.py:86
  10.0 0.6 select_bitcast_fusion
  10.6 0.7 and_select_fusion
  11.3 1.1 %collective-permute-done.1.rest_2_ = bf16[15,128,128]{2,1,0:T(8,128)(2,1)S(1)} collective-permute-done((bf16[15,128,128]{2,1,0:T(8,128)(2,1)}, bf16[15,128,128]{2,1,0:T(8,128)(2,1)S(1)}, u32[]{:S(2)}, u32[]{:S(2)}) %collective-permute-start.1) | collective-permute-done | bytes 491552 | tf_op jit(solution)/shard_map/ppermute | solution.py:319
  12.3 1.5 %collective-permute-start.2 = (bf16[15,128,128]{2,1,0:T(8,128)(2,1)S(1)}, bf16[15,128,128]{2,1,0:T(8,128)(2,1)S(1)}, u32[]{:S(2)}, u32[]{:S(2)}) collective-permute-start(bf16[15,128,128]{2,1,0:T(8,128)(2,1)S(1)} %collective-permute-done.1.rest_2_), channel_id=1, source_target_pairs={{0,8},{8,0},{16,24},{24,16},{1,9},{9,1},{17,25},{25,17},{2,10},{10... | collective-permute-start | bytes 1474568 | tf_op jit(solution)/shard_map/ppermute | solution.py:321
  14.6 4.9 %sort.7.keys_ref = s32[2432]{0:T(1024)S(1)} sort(s32[2432]{0:T(1024)S(1)} %pad_add_fusion), dimensions={0}, to_apply=%region_3.4 | sort | flops 29184 | bytes 19456 | tf_op jit(solution)/shard_map/sort | solution.py:92
  19.5 0.9 convert_reduce_fusion.1.place_ref
  20.4 0.2 select_reduce_fusion
  20.6 0.1 reshape.48
  20.7 0.0 copy-start
  20.7 3.4 %copy-done = bf16[256,128,128]{2,1,0:T(8,128)(2,1)S(1)} copy-done((bf16[256,128,128]{2,1,0:T(8,128)(2,1)S(1)}, bf16[256,128,128]{2,1,0:T(8,128)(2,1)}, u32[]{:S(2)}) %copy-start) | copy-done | bytes 8388632
  24.1 1.0 %copy-done.2 = bf16[15,128,128]{2,1,0:T(8,128)(2,1)S(1)} copy-done((bf16[15,128,128]{2,1,0:T(8,128)(2,1)S(1)}, bf16[15,128,128]{2,1,0:T(8,128)(2,1)}, u32[]{:S(2)}) %copy-start.2) | copy-done | bytes 491544
  25.1 19.1 %shard_map.73.part = f32[128,128,128]{2,1,0:T(8,128)S(1)} custom-call(s32[1]{0:T(128)} %bitcast.n_ref, s32[2432]{0:T(1024)S(1)} %sort.7.keys_ref, s32[128]{0:T(128)S(1)} %convert_reduce_fusion.1.place_ref, s32[4]{0:T(128)S(1)} %iota_xor_fusion.groups_ref, bf16[256,128,128]{2,1,0:T(8,128)(2,1)S(1)} %copy-done, bf16[15,128,128]{2,1,0:T(8,128)(2,1)S(1)} %copy-done.2, ...), custom_call_target="tpu_custom_call" | custom-call | tf_op jit(solution)/shard_map/pallas_call | solution.py:60
  44.3 51.6 %shard_map.74 = (s16[32,128,128]{2,1,0:T(8,128)(2,1)S(1)}, f32[8,8,128]{2,1,0:T(8,128)S(1)}) custom-call(f32[128,128,128]{2,1,0:T(8,128)S(1)} %shard_map.73.part, f32[8,8,128]{2,1,0:T(8,128)S(1)} %pad_convert_fusion.pos_ref), custom_call_target="tpu_custom_call" | custom-call | tf_op jit(solution)/shard_map/pallas_call | solution.py:256
  95.9 1.0 copy-done.1
  96.9 0.6 convert_element_type.21.target_ref
  97.5 2.5 %shard_map.75 = f32[32,128,128]{2,1,0:T(8,128)} custom-call(s32[32]{0:T(128)} %convert_element_type.21.target_ref, s16[32,128,128]{2,1,0:T(8,128)(2,1)} %copy-done.1, f32[8,8,128]{2,1,0:T(8,128)} %copy-done.3), custom_call_target="tpu_custom_call" | custom-call | tf_op jit(solution)/shard_map/pallas_call | solution.py:301
  (11 shorter events, 0.1 us)
Async XLA Ops:
  0.0 12.3 %collective-permute-start.1 = (bf16[15,128,128]{2,1,0:T(8,128)(2,1)}, bf16[15,128,128]{2,1,0:T(8,128)(2,1)S(1)}, u32[]{:S(2)}, u32[]{:S(2)}) collective-permute-start(bf16[15,128,128]{2,1,0:T(8,128)(2,1)} %rest_0_.1), channel_id=1, source_target_pairs={{0,16},{8,24},{16,0},{24,8},{1,17},{9,25},{17,1},{25,9},{2,18},{10... | collective-permute-start | bytes 1474568 | tf_op jit(solution)/shard_map/ppermute | solution.py:319
  1.2 19.4 %collective-permute-start = (bf16[15,128,128]{2,1,0:T(8,128)(2,1)}, bf16[15,128,128]{2,1,0:T(8,128)(2,1)S(1)}, u32[]{:S(2)}, u32[]{:S(2)}) collective-permute-start(bf16[15,128,128]{2,1,0:T(8,128)(2,1)} %rest_0_.1), channel_id=1, source_target_pairs={{0,8},{8,0},{16,24},{24,16},{1,9},{9,1},{17,25},{25,17},{2,10},{10... | collective-permute-start | bytes 1474568 | tf_op jit(solution)/shard_map/ppermute | solution.py:320
  12.3 8.4 %collective-permute-start.2 = (bf16[15,128,128]{2,1,0:T(8,128)(2,1)S(1)}, bf16[15,128,128]{2,1,0:T(8,128)(2,1)S(1)}, u32[]{:S(2)}, u32[]{:S(2)}) collective-permute-start(bf16[15,128,128]{2,1,0:T(8,128)(2,1)S(1)} %collective-permute-done.1.rest_2_), channel_id=1, source_target_pairs={{0,8},{8,0},{16,24},{24,16},{1,9},{9,1},{17,25},{25,17},{2,10},{10... | collective-permute-start | bytes 1474568 | tf_op jit(solution)/shard_map/ppermute | solution.py:321
  20.7 3.4 %copy-start = (bf16[256,128,128]{2,1,0:T(8,128)(2,1)S(1)}, bf16[256,128,128]{2,1,0:T(8,128)(2,1)}, u32[]{:S(2)}) copy-start(bf16[256,128,128]{2,1,0:T(8,128)(2,1)} %ints.1) | copy-start | bytes 25165828
  24.1 1.0 %copy-start.2 = (bf16[15,128,128]{2,1,0:T(8,128)(2,1)S(1)}, bf16[15,128,128]{2,1,0:T(8,128)(2,1)}, u32[]{:S(2)}) copy-start(bf16[15,128,128]{2,1,0:T(8,128)(2,1)} %rest_0_.1) | copy-start | bytes 1474564
  95.9 1.0 copy-start.1
  96.9 0.6 copy-start.3

commit v5 on v4

--- a/solution.py
+++ b/solution.py
@@ -6,7 +6,7 @@
 from jax.sharding import PartitionSpec as P
 
 CHUNK = 4
-UNROLL = 8
+UNROLL = 16
 STEPS = 8
 LAG = 1
 MESH = pl.DeviceIdType.MESH
@@ -22,14 +22,15 @@
     st_mask = (1 << st_bits) - 1
     blk_mask = (1 << blk_bits) - 1
 
-    def kernel(n_ref, keys_ref, place_ref, groups_ref, ints, *rest):
-        den_refs, (acc, dens, sems) = rest[:len(pieces)], rest[len(pieces):]
+    def kernel(n_ref, keys_ref, place_ref, groups_ref, int_hbm, *rest):
+        den_refs, (acc, ints, dens, sems) = rest[:len(pieces)], rest[len(pieces):]
         loads = [
             pltpu.make_async_copy(
                 ref, dens.at[pl.ds(groups_ref[i] * s_group, s_group)], sems.at[i]
             )
             for i, ref in enumerate(den_refs)
         ]
+        loads.append(pltpu.make_async_copy(int_hbm, ints, sems.at[len(pieces)]))
         for load in loads:
             load.start()
         dens[states] = jnp.zeros((size, size), dens.dtype)
@@ -60,13 +61,14 @@
     return pl.pallas_call(
         kernel,
         out_shape=jax.ShapeDtypeStruct((hb_rows, size, size), jnp.float32),
-        in_specs=[smem] * 4 + [vmem] + [hbm] * len(pieces),
+        in_specs=[smem] * 4 + [hbm] * (1 + len(pieces)),
         out_specs=vmem,
         scratch_shapes=[
+            pltpu.VMEM(integrals.shape, integrals.dtype),
             pltpu.VMEM((states + 1, size, size), pieces[0].dtype),
-            pltpu.SemaphoreType.DMA((len(pieces),)),
+            pltpu.SemaphoreType.DMA((len(pieces) + 1,)),
         ],
-        compiler_params=pltpu.CompilerParams(vmem_limit_bytes=32 << 20),
+        compiler_params=pltpu.CompilerParams(vmem_limit_bytes=40 << 20),
     )(n_steps, keys, place, groups, integrals, *pieces)
 
 
@@ -192,7 +194,6 @@
 
         for i in range(steps):
             first(i, 1).start()
-            first(i, 0).start()
 
         def finish(i):
             first(i, 0).wait_recv()
@@ -221,6 +222,7 @@
                     third_steps(dest, b).start()
 
         for i in range(steps):
+            first(i, 0).start()
             first(i, 1).wait_recv()
             for k in range(rows):
                 row = span(i) + k
@@ -260,7 +262,7 @@
             jax.ShapeDtypeStruct(pos.shape, jnp.float32),
         ),
         in_specs=[vmem, vmem],
-        out_specs=(vmem, vmem),
+        out_specs=(pl.BlockSpec(memory_space=pltpu.HBM),) * 2,
         scratch_shapes=[
             pltpu.VMEM((2,) + block, jnp.float32),
             pltpu.VMEM(block, jnp.int16),

time: 101 us -> 93.8 us (0.929); the launches traced: 100 us -> 94.1 us
  local copies, waits for them, and re-layouts: 6.66 us -> 3.28 us
  Pallas kernels: 73.3 us -> 70.7 us
    pallas_call x1, Pallas kernels: 19.1 us -> 11 us  [accumulate(): pl.pallas_call(kernel, out_shape=jax.ShapeDtypeStruct((hb_rows, size, siz...]
    pallas_call x1, Pallas kernels: 51.6 us -> 57.1 us  [exchange(): pl.pallas_call(kernel, out_shape=(jax.ShapeDtypeStruct(block, jnp.int16),...]
    unnamed x8 -> x6, local copies, waits for them, and re-layouts: 5.39 us -> 2.01 us
  transfers between devices with their start and end apart: 3 -> 3, of which waited for: 1 -> 1; matrix products, arithmetic and copies ran while one was open for 15% -> 16% of each run, Pallas kernels for 0% -> 0%
where the time goes in v5:
time: 93.8 us; the launch traced here: 94.1 us
  Pallas kernels  70.7 us (75%)
  other arithmetic  14.5 us (15%)
  starting transfers between devices  3.74 us (4%)
  local copies, waits for them, and re-layouts  3.28 us (3%)
  waiting for transfers between devices  1.06 us (1%)
    pallas_call x1, Pallas kernels, exchange(): pl.pallas_call(kernel, out_shape=(jax.ShapeDtypeStruct(block, jnp.int16),...  57.1 us
    pallas_call x1, Pallas kernels, accumulate(): pl.pallas_call(kernel, out_shape=jax.ShapeDtypeStruct((hb_rows, size, siz...  11 us
    sort x1, other arithmetic, make_keys(): keys = lax.sort(jnp.concatenate([key, fill, tail]), is_stable=False)  4.9 us
    reduce_sum x1, other arithmetic, make_keys(): jnp.sum(((entry_slot[:, None] == slots[None, :]) & valid[:, None]).astype...  2.62 us
    pallas_call x1, Pallas kernels, arrange(): pl.pallas_call(kernel, out_shape=jax.ShapeDtypeStruct(blocks.shape, jnp.f...  2.53 us
    unnamed x6, local copies, waits for them, and re-layouts  2.01 us
    select_n x1, other arithmetic, make_keys(): key = jnp.where(valid, key, last)  1.94 us
  transfers between devices with their start and end apart: 3, of which 1 were waited for; matrix products, arithmetic and copies ran while one was open for 16% of the time, Pallas kernels for 0%

profile of v5, /device:TPU:11, one launch (start us, length us, event | category | flops | bytes accessed | tf_op | source)
XLA Modules:
  0.0 94.1 jit_solution(9025877705835765239)
XLA Ops:
  0.0 1.2 %collective-permute-start.1 = (bf16[15,128,128]{2,1,0:T(8,128)(2,1)}, bf16[15,128,128]{2,1,0:T(8,128)(2,1)S(1)}, u32[]{:S(2)}, u32[]{:S(2)}) collective-permute-start(bf16[15,128,128]{2,1,0:T(8,128)(2,1)} %rest_0_.1), channel_id=1, source_target_pairs={{0,16},{8,24},{16,0},{24,8},{1,17},{9,25},{17,1},{25,9},{2,18},{10... | collective-permute-start | bytes 1474568 | tf_op jit(solution)/shard_map/ppermute | solution.py:321
  1.2 1.0 %collective-permute-start = (bf16[15,128,128]{2,1,0:T(8,128)(2,1)}, bf16[15,128,128]{2,1,0:T(8,128)(2,1)S(1)}, u32[]{:S(2)}, u32[]{:S(2)}) collective-permute-start(bf16[15,128,128]{2,1,0:T(8,128)(2,1)} %rest_0_.1), channel_id=1, source_target_pairs={{0,8},{8,0},{16,24},{24,16},{1,9},{9,1},{17,25},{25,17},{2,10},{10... | collective-permute-start | bytes 1474568 | tf_op jit(solution)/shard_map/ppermute | solution.py:322
  2.2 1.3 %reduce_sum.45 = s32[]{:T(128)} reduce(s32[1,4]{1,0:T(1,128)} %param.12, s32[]{:T(128)} %constant.49.clone.1), dimensions={0,1}, to_apply=%region_0.0 | reduce | flops 3 | bytes 24 | tf_op jit(solution)/shard_map/reduce_sum | solution.py:327
  3.5 0.7 iota_compare_fusion.1
  4.1 2.6 %convert_reduce_fusion = s32[128]{0:T(128)S(1)} fusion(s32[2048]{0:T(1024)} %param.11, pred[2048]{0:T(1024)(128)(4,1)S(1)} %iota_compare_fusion.1), kind=kLoop, calls=%fused_computation | loop fusion | flops 1048448 | bytes 10752 | tf_op jit(solution)/shard_map/reduce_sum | solution.py:81
  6.8 0.7 add_reduce_fusion
  7.5 0.6 slice.6
  8.1 1.9 %add_select_fusion = s32[2048]{0:T(1024)S(1)} fusion(s32[2048]{0:T(1024)} %param.10, s32[2048]{0:T(1024)} %param.9, s32[2048]{0:T(1024)} %param.11, s32[]{:T(128)} %bitcast.1, s32[]{:T(128)} %reduce_sum.45), kind=kLoop, calls=%fused_computation.7 | loop fusion | flops 12288 | bytes 32776 | tf_op jit(solution)/shard_map/jit(_where)/select_n | solution.py:88
  10.0 0.6 select_bitcast_fusion
  10.6 0.7 and_select_fusion
  11.3 1.1 %collective-permute-done.1.rest_2_ = bf16[15,128,128]{2,1,0:T(8,128)(2,1)S(1)} collective-permute-done((bf16[15,128,128]{2,1,0:T(8,128)(2,1)}, bf16[15,128,128]{2,1,0:T(8,128)(2,1)S(1)}, u32[]{:S(2)}, u32[]{:S(2)}) %collective-permute-start.1) | collective-permute-done | bytes 491552 | tf_op jit(solution)/shard_map/ppermute | solution.py:321
  12.3 1.5 %collective-permute-start.2 = (bf16[15,128,128]{2,1,0:T(8,128)(2,1)S(1)}, bf16[15,128,128]{2,1,0:T(8,128)(2,1)S(1)}, u32[]{:S(2)}, u32[]{:S(2)}) collective-permute-start(bf16[15,128,128]{2,1,0:T(8,128)(2,1)S(1)} %collective-permute-done.1.rest_2_), channel_id=1, source_target_pairs={{0,8},{8,0},{16,24},{24,16},{1,9},{9,1},{17,25},{25,17},{2,10},{10... | collective-permute-start | bytes 1474568 | tf_op jit(solution)/shard_map/ppermute | solution.py:323
  14.6 4.9 %sort.7.keys_ref = s32[2432]{0:T(1024)S(1)} sort(s32[2432]{0:T(1024)S(1)} %pad_add_fusion), dimensions={0}, to_apply=%region_3.4 | sort | flops 29184 | bytes 19456 | tf_op jit(solution)/shard_map/sort | solution.py:94
  19.5 0.9 convert_reduce_fusion.1.place_ref
  20.4 0.2 select_reduce_fusion
  20.6 0.1 reshape.48
  20.7 0.0 collective-permute-done.rest_1_
  20.7 0.0 copy-start.1
  20.7 1.0 %copy-done.1 = bf16[15,128,128]{2,1,0:T(8,128)(2,1)S(1)} copy-done((bf16[15,128,128]{2,1,0:T(8,128)(2,1)S(1)}, bf16[15,128,128]{2,1,0:T(8,128)(2,1)}, u32[]{:S(2)}) %copy-start.1) | copy-done | bytes 491544
  21.7 11.0 %shard_map.73.part = f32[128,128,128]{2,1,0:T(8,128)S(1)} custom-call(s32[1]{0:T(128)} %bitcast.n_ref, s32[2432]{0:T(1024)S(1)} %sort.7.keys_ref, s32[128]{0:T(128)S(1)} %convert_reduce_fusion.1.place_ref, s32[4]{0:T(128)S(1)} %iota_xor_fusion.groups_ref, bf16[256,128,128]{2,1,0:T(8,128)(2,1)} %int_hbm.1, bf16[15,128,128]{2,1,0:T(8,128)(2,1)S(1)} %copy-done.1, ...), custom_call_target="tpu_custom_call" | custom-call | tf_op jit(solution)/shard_map/pallas_call | solution.py:61
  32.7 57.1 %shard_map.74 = (s16[32,128,128]{2,1,0:T(8,128)(2,1)S(1)}, f32[8,8,128]{2,1,0:T(8,128)S(1)}) custom-call(f32[128,128,128]{2,1,0:T(8,128)S(1)} %shard_map.73.part, f32[8,8,128]{2,1,0:T(8,128)S(1)} %pad_convert_fusion.pos_ref), custom_call_target="tpu_custom_call" | custom-call | tf_op jit(solution)/shard_map/pallas_call | solution.py:258
  89.9 1.0 %copy-done = s16[32,128,128]{2,1,0:T(8,128)(2,1)} copy-done((s16[32,128,128]{2,1,0:T(8,128)(2,1)}, s16[32,128,128]{2,1,0:T(8,128)(2,1)S(1)}, u32[]{:S(2)}) %copy-start) | copy-done | bytes 1048600
  90.9 0.6 convert_element_type.21.target_ref
  91.5 2.5 %shard_map.75 = f32[32,128,128]{2,1,0:T(8,128)} custom-call(s32[32]{0:T(128)} %convert_element_type.21.target_ref, s16[32,128,128]{2,1,0:T(8,128)(2,1)} %copy-done, f32[8,8,128]{2,1,0:T(8,128)} %copy-done.2), custom_call_target="tpu_custom_call" | custom-call | tf_op jit(solution)/shard_map/pallas_call | solution.py:303
  (9 shorter events, 0.1 us)
Async XLA Ops:
  0.0 12.3 %collective-permute-start.1 = (bf16[15,128,128]{2,1,0:T(8,128)(2,1)}, bf16[15,128,128]{2,1,0:T(8,128)(2,1)S(1)}, u32[]{:S(2)}, u32[]{:S(2)}) collective-permute-start(bf16[15,128,128]{2,1,0:T(8,128)(2,1)} %rest_0_.1), channel_id=1, source_target_pairs={{0,16},{8,24},{16,0},{24,8},{1,17},{9,25},{17,1},{25,9},{2,18},{10... | collective-permute-start | bytes 1474568 | tf_op jit(solution)/shard_map/ppermute | solution.py:321
  1.2 19.4 %collective-permute-start = (bf16[15,128,128]{2,1,0:T(8,128)(2,1)}, bf16[15,128,128]{2,1,0:T(8,128)(2,1)S(1)}, u32[]{:S(2)}, u32[]{:S(2)}) collective-permute-start(bf16[15,128,128]{2,1,0:T(8,128)(2,1)} %rest_0_.1), channel_id=1, source_target_pairs={{0,8},{8,0},{16,24},{24,16},{1,9},{9,1},{17,25},{25,17},{2,10},{10... | collective-permute-start | bytes 1474568 | tf_op jit(solution)/shard_map/ppermute | solution.py:322
  12.3 8.4 %collective-permute-start.2 = (bf16[15,128,128]{2,1,0:T(8,128)(2,1)S(1)}, bf16[15,128,128]{2,1,0:T(8,128)(2,1)S(1)}, u32[]{:S(2)}, u32[]{:S(2)}) collective-permute-start(bf16[15,128,128]{2,1,0:T(8,128)(2,1)S(1)} %collective-permute-done.1.rest_2_), channel_id=1, source_target_pairs={{0,8},{8,0},{16,24},{24,16},{1,9},{9,1},{17,25},{25,17},{2,10},{10... | collective-permute-start | bytes 1474568 | tf_op jit(solution)/shard_map/ppermute | solution.py:323
  20.7 1.0 %copy-start.1 = (bf16[15,128,128]{2,1,0:T(8,128)(2,1)S(1)}, bf16[15,128,128]{2,1,0:T(8,128)(2,1)}, u32[]{:S(2)}) copy-start(bf16[15,128,128]{2,1,0:T(8,128)(2,1)} %rest_0_.1) | copy-start | bytes 1474564
  89.9 1.0 %copy-start = (s16[32,128,128]{2,1,0:T(8,128)(2,1)}, s16[32,128,128]{2,1,0:T(8,128)(2,1)S(1)}, u32[]{:S(2)}) copy-start(s16[32,128,128]{2,1,0:T(8,128)(2,1)S(1)} %get-tuple-element.8.src) | copy-start | bytes 3145732
  90.9 0.6 copy-start.2

commit v6 on v5

--- a/solution.py
+++ b/solution.py
@@ -8,7 +8,7 @@
 CHUNK = 4
 UNROLL = 16
 STEPS = 8
-LAG = 1
+LAG = 2
 MESH = pl.DeviceIdType.MESH
 
 

time: 93.8 us -> 93.9 us (level)
    pallas_call x1, Pallas kernels: 57.1 us -> 49.7 us  [exchange(): pl.pallas_call(kernel, out_shape=(jax.ShapeDtypeStruct(block, jnp.int16),...]
    pallas_call x1, Pallas kernels: 11 us -> 18 us  [accumulate(): pl.pallas_call(kernel, out_shape=jax.ShapeDtypeStruct((hb_rows, size, siz...]
where the time goes in v6:
time: 93.9 us; the launch traced here: 93.7 us
  Pallas kernels  70.3 us (75%)
  other arithmetic  14.5 us (15%)
  starting transfers between devices  3.74 us (4%)
  local copies, waits for them, and re-layouts  3.28 us (3%)
  waiting for transfers between devices  1.06 us (1%)
    pallas_call x1, Pallas kernels, exchange(): pl.pallas_call(kernel, out_shape=(jax.ShapeDtypeStruct(block, jnp.int16),...  49.7 us
    pallas_call x1, Pallas kernels, accumulate(): pl.pallas_call(kernel, out_shape=jax.ShapeDtypeStruct((hb_rows, size, siz...  18 us
    sort x1, other arithmetic, make_keys(): keys = lax.sort(jnp.concatenate([key, fill, tail]), is_stable=False)  4.9 us
    reduce_sum x1, other arithmetic, make_keys(): jnp.sum(((entry_slot[:, None] == slots[None, :]) & valid[:, None]).astype...  2.62 us
    pallas_call x1, Pallas kernels, arrange(): pl.pallas_call(kernel, out_shape=jax.ShapeDtypeStruct(blocks.shape, jnp.f...  2.53 us
    unnamed x6, local copies, waits for them, and re-layouts  2.01 us
    select_n x1, other arithmetic, make_keys(): key = jnp.where(valid, key, last)  1.94 us
  transfers between devices with their start and end apart: 3, of which 1 were waited for; matrix products, arithmetic and copies ran while one was open for 16% of the time, Pallas kernels for 0%

profile of v6, /device:TPU:11, one launch (start us, length us, event | category | flops | bytes accessed | tf_op | source)
XLA Modules:
  0.0 93.7 jit_solution(17577714107958597443)
XLA Ops:
  0.0 1.2 %collective-permute-start.1 = (bf16[15,128,128]{2,1,0:T(8,128)(2,1)}, bf16[15,128,128]{2,1,0:T(8,128)(2,1)S(1)}, u32[]{:S(2)}, u32[]{:S(2)}) collective-permute-start(bf16[15,128,128]{2,1,0:T(8,128)(2,1)} %rest_0_.1), channel_id=1, source_target_pairs={{0,16},{8,24},{16,0},{24,8},{1,17},{9,25},{17,1},{25,9},{2,18},{10... | collective-permute-start | bytes 1474568 | tf_op jit(solution)/shard_map/ppermute | solution.py:321
  1.2 1.0 %collective-permute-start = (bf16[15,128,128]{2,1,0:T(8,128)(2,1)}, bf16[15,128,128]{2,1,0:T(8,128)(2,1)S(1)}, u32[]{:S(2)}, u32[]{:S(2)}) collective-permute-start(bf16[15,128,128]{2,1,0:T(8,128)(2,1)} %rest_0_.1), channel_id=1, source_target_pairs={{0,8},{8,0},{16,24},{24,16},{1,9},{9,1},{17,25},{25,17},{2,10},{10... | collective-permute-start | bytes 1474568 | tf_op jit(solution)/shard_map/ppermute | solution.py:322
  2.2 1.3 %reduce_sum.45 = s32[]{:T(128)} reduce(s32[1,4]{1,0:T(1,128)} %param.12, s32[]{:T(128)} %constant.49.clone.1), dimensions={0,1}, to_apply=%region_0.0 | reduce | flops 3 | bytes 24 | tf_op jit(solution)/shard_map/reduce_sum | solution.py:327
  3.5 0.7 iota_compare_fusion.1
  4.1 2.6 %convert_reduce_fusion = s32[128]{0:T(128)S(1)} fusion(s32[2048]{0:T(1024)} %param.11, pred[2048]{0:T(1024)(128)(4,1)S(1)} %iota_compare_fusion.1), kind=kLoop, calls=%fused_computation | loop fusion | flops 1048448 | bytes 10752 | tf_op jit(solution)/shard_map/reduce_sum | solution.py:81
  6.8 0.7 add_reduce_fusion
  7.5 0.6 slice.6
  8.1 1.9 %add_select_fusion = s32[2048]{0:T(1024)S(1)} fusion(s32[2048]{0:T(1024)} %param.10, s32[2048]{0:T(1024)} %param.9, s32[2048]{0:T(1024)} %param.11, s32[]{:T(128)} %bitcast.1, s32[]{:T(128)} %reduce_sum.45), kind=kLoop, calls=%fused_computation.7 | loop fusion | flops 12288 | bytes 32776 | tf_op jit(solution)/shard_map/jit(_where)/select_n | solution.py:88
  10.0 0.6 select_bitcast_fusion
  10.6 0.7 and_select_fusion
  11.3 1.1 %collective-permute-done.1.rest_2_ = bf16[15,128,128]{2,1,0:T(8,128)(2,1)S(1)} collective-permute-done((bf16[15,128,128]{2,1,0:T(8,128)(2,1)}, bf16[15,128,128]{2,1,0:T(8,128)(2,1)S(1)}, u32[]{:S(2)}, u32[]{:S(2)}) %collective-permute-start.1) | collective-permute-done | bytes 491552 | tf_op jit(solution)/shard_map/ppermute | solution.py:321
  12.3 1.5 %collective-permute-start.2 = (bf16[15,128,128]{2,1,0:T(8,128)(2,1)S(1)}, bf16[15,128,128]{2,1,0:T(8,128)(2,1)S(1)}, u32[]{:S(2)}, u32[]{:S(2)}) collective-permute-start(bf16[15,128,128]{2,1,0:T(8,128)(2,1)S(1)} %collective-permute-done.1.rest_2_), channel_id=1, source_target_pairs={{0,8},{8,0},{16,24},{24,16},{1,9},{9,1},{17,25},{25,17},{2,10},{10... | collective-permute-start | bytes 1474568 | tf_op jit(solution)/shard_map/ppermute | solution.py:323
  14.6 4.9 %sort.7.keys_ref = s32[2432]{0:T(1024)S(1)} sort(s32[2432]{0:T(1024)S(1)} %pad_add_fusion), dimensions={0}, to_apply=%region_3.4 | sort | flops 29184 | bytes 19456 | tf_op jit(solution)/shard_map/sort | solution.py:94
  19.5 0.9 convert_reduce_fusion.1.place_ref
  20.4 0.2 select_reduce_fusion
  20.6 0.1 reshape.48
  20.7 0.0 collective-permute-done.rest_1_
  20.7 0.0 copy-start.1
  20.7 1.0 %copy-done.1 = bf16[15,128,128]{2,1,0:T(8,128)(2,1)S(1)} copy-done((bf16[15,128,128]{2,1,0:T(8,128)(2,1)S(1)}, bf16[15,128,128]{2,1,0:T(8,128)(2,1)}, u32[]{:S(2)}) %copy-start.1) | copy-done | bytes 491544
  21.7 18.0 %shard_map.73.part = f32[128,128,128]{2,1,0:T(8,128)S(1)} custom-call(s32[1]{0:T(128)} %bitcast.n_ref, s32[2432]{0:T(1024)S(1)} %sort.7.keys_ref, s32[128]{0:T(128)S(1)} %convert_reduce_fusion.1.place_ref, s32[4]{0:T(128)S(1)} %iota_xor_fusion.groups_ref, bf16[256,128,128]{2,1,0:T(8,128)(2,1)} %int_hbm.1, bf16[15,128,128]{2,1,0:T(8,128)(2,1)S(1)} %copy-done.1, ...), custom_call_target="tpu_custom_call" | custom-call | tf_op jit(solution)/shard_map/pallas_call | solution.py:61
  39.7 49.7 %shard_map.74 = (s16[32,128,128]{2,1,0:T(8,128)(2,1)S(1)}, f32[8,8,128]{2,1,0:T(8,128)S(1)}) custom-call(f32[128,128,128]{2,1,0:T(8,128)S(1)} %shard_map.73.part, f32[8,8,128]{2,1,0:T(8,128)S(1)} %pad_convert_fusion.pos_ref), custom_call_target="tpu_custom_call" | custom-call | tf_op jit(solution)/shard_map/pallas_call | solution.py:258
  89.5 1.0 %copy-done = s16[32,128,128]{2,1,0:T(8,128)(2,1)} copy-done((s16[32,128,128]{2,1,0:T(8,128)(2,1)}, s16[32,128,128]{2,1,0:T(8,128)(2,1)S(1)}, u32[]{:S(2)}) %copy-start) | copy-done | bytes 1048600
  90.5 0.6 convert_element_type.21.target_ref
  91.1 2.5 %shard_map.75 = f32[32,128,128]{2,1,0:T(8,128)} custom-call(s32[32]{0:T(128)} %convert_element_type.21.target_ref, s16[32,128,128]{2,1,0:T(8,128)(2,1)} %copy-done, f32[8,8,128]{2,1,0:T(8,128)} %copy-done.2), custom_call_target="tpu_custom_call" | custom-call | tf_op jit(solution)/shard_map/pallas_call | solution.py:303
  (9 shorter events, 0.1 us)
Async XLA Ops:
  0.0 12.3 %collective-permute-start.1 = (bf16[15,128,128]{2,1,0:T(8,128)(2,1)}, bf16[15,128,128]{2,1,0:T(8,128)(2,1)S(1)}, u32[]{:S(2)}, u32[]{:S(2)}) collective-permute-start(bf16[15,128,128]{2,1,0:T(8,128)(2,1)} %rest_0_.1), channel_id=1, source_target_pairs={{0,16},{8,24},{16,0},{24,8},{1,17},{9,25},{17,1},{25,9},{2,18},{10... | collective-permute-start | bytes 1474568 | tf_op jit(solution)/shard_map/ppermute | solution.py:321
  1.2 19.4 %collective-permute-start = (bf16[15,128,128]{2,1,0:T(8,128)(2,1)}, bf16[15,128,128]{2,1,0:T(8,128)(2,1)S(1)}, u32[]{:S(2)}, u32[]{:S(2)}) collective-permute-start(bf16[15,128,128]{2,1,0:T(8,128)(2,1)} %rest_0_.1), channel_id=1, source_target_pairs={{0,8},{8,0},{16,24},{24,16},{1,9},{9,1},{17,25},{25,17},{2,10},{10... | collective-permute-start | bytes 1474568 | tf_op jit(solution)/shard_map/ppermute | solution.py:322
  12.3 8.4 %collective-permute-start.2 = (bf16[15,128,128]{2,1,0:T(8,128)(2,1)S(1)}, bf16[15,128,128]{2,1,0:T(8,128)(2,1)S(1)}, u32[]{:S(2)}, u32[]{:S(2)}) collective-permute-start(bf16[15,128,128]{2,1,0:T(8,128)(2,1)S(1)} %collective-permute-done.1.rest_2_), channel_id=1, source_target_pairs={{0,8},{8,0},{16,24},{24,16},{1,9},{9,1},{17,25},{25,17},{2,10},{10... | collective-permute-start | bytes 1474568 | tf_op jit(solution)/shard_map/ppermute | solution.py:323
  20.7 1.0 %copy-start.1 = (bf16[15,128,128]{2,1,0:T(8,128)(2,1)S(1)}, bf16[15,128,128]{2,1,0:T(8,128)(2,1)}, u32[]{:S(2)}) copy-start(bf16[15,128,128]{2,1,0:T(8,128)(2,1)} %rest_0_.1) | copy-start | bytes 1474564
  89.5 1.0 %copy-start = (s16[32,128,128]{2,1,0:T(8,128)(2,1)}, s16[32,128,128]{2,1,0:T(8,128)(2,1)S(1)}, u32[]{:S(2)}) copy-start(s16[32,128,128]{2,1,0:T(8,128)(2,1)S(1)} %get-tuple-element.8.src) | copy-start | bytes 3145732
  90.5 0.6 copy-start.2
